TPU v7x, 32 devices: a whole 2x2x4 slice. The times are simulated.
32 devices in a mesh: rhombus: 4 (over z), tile: 8 (over y, x, core).
Axes of the slice: x: 2, y: 2, z: 4, core: 2. Of those that a mesh axis runs over, the one named last changes fastest.
Arguments:
- fine_latent: bfloat16 [16384, 512], P(('rhombus', 'tile')), may hold values from -6 to 6
- mid_latent: bfloat16 [1024, 512], P(('rhombus', 'tile')), may hold values from -6 to 6
- coarse_latent: bfloat16 [642, 512], replicated, may hold values from -6 to 6
- fine_parent: int32 [16384], P(('rhombus', 'tile')), may hold values from 0 to 95, as said below
- mid_parent: int32 [1024], P(('rhombus', 'tile')), may hold values from 0 to 641
- halo_rows: int32 [8192], P(('rhombus', 'tile')), may hold values from 0 to 511
- edge_source: int32 [98304], P(('rhombus', 'tile')), may hold values from 0 to 767
- edge_target: int32 [98304], P(('rhombus', 'tile')), may hold values from 0 to 512, as said below
- w_child: bfloat16 [512, 512], replicated, may hold values from -1 to 1
- mid_w1: bfloat16 [512, 512], replicated, may hold values from -0.25 to 0.25
- mid_w2: bfloat16 [512, 512], replicated, may hold values from -0.5 to 0.5
- mid_w3: bfloat16 [512, 512], replicated, may hold values from -0.25 to 0.25
- w_coarse: bfloat16 [512, 512], replicated, may hold values from -1 to 1
- coarse_w1: bfloat16 [512, 512], replicated, may hold values from -0.25 to 0.25
- coarse_w2: bfloat16 [512, 512], replicated, may hold values from -0.5 to 0.5
- coarse_w3: bfloat16 [512, 512], replicated, may hold values from -0.25 to 0.25
- w_descend: bfloat16 [512, 512], replicated, may hold values from -0.25 to 0.25
- w_fine: bfloat16 [512, 512], replicated, may hold values from -0.25 to 0.25
- edge_w_src: bfloat16 [512, 512], replicated, may hold values from -1 to 1
- edge_w_dst: bfloat16 [512, 512], replicated, may hold values from -0.25 to 0.25
- edge_w2: bfloat16 [512, 512], replicated, may hold values from -0.25 to 0.25
- node_w1: bfloat16 [512, 512], replicated, may hold values from -0.25 to 0.25
- node_w2: bfloat16 [512, 512], replicated, may hold values from -0.125 to 0.125
- node_w3: bfloat16 [512, 512], replicated, may hold values from -0.25 to 0.25
Outputs:
- fine_out: bfloat16 [16384, 512], P(('rhombus', 'tile'))
- mid_out: bfloat16 [1024, 512], P(('rhombus', 'tile'))
- coarse_out: bfloat16 [642, 512], replicated
Inputs may be any that keep to these rules, and one draw needn't show every extreme that they name: `fine_parent`: in tile t of a group, an entry p < 32 names a middle slot of the same tile, 32 <= p < 64 a slot of tile t - 1, 64 <= p a slot of tile t + 1; tile 0 never names the tile before and the last tile of a group never names the tile after. `edge_target`: in each tile the live slots come first and name a fine row of that tile; the remaining slots hold 512. Each tile has at least 1536 live slots, and some tile has all 3072 slots live.
All inputs are finite; a program needn't handle non-finite values.
Results may differ from a plain program's by a relative error of at most 0.013.
Values may be sent and summed in bfloat16 or wider, within the bound.
A program may use at most 64 MiB of HBM per device.

v0:
```python
import jax
import jax.numpy as jnp
from jax import lax
from jax.sharding import PartitionSpec as P

EPSILON = 1e-05


def extended_2(shard, sides, width):
    for axis, dim in sides:
        size, length = (lax.axis_size(axis), shard.shape[dim])
        up = [(i, (i + 1) % size) for i in range(size - 1)]
        down = [(j, i) for i, j in up]
        last = lax.slice_in_dim(shard, length - width, length, axis=dim)
        leading = lax.slice_in_dim(shard, 0, width, axis=dim)
        before = lax.ppermute(last, axis, up)
        after = lax.ppermute(leading, axis, down)
        shard = jnp.concatenate([before, shard, after], axis=dim)
    return shard


def product(left, right):
    return jnp.dot(left, right, preferred_element_type=jnp.float32)


def normed(values):
    return values / jnp.sqrt(jnp.mean(values * values, axis=-1, keepdims=True) + EPSILON)


def node_update(latent, incoming, first, second, third):
    hidden = jax.nn.silu(product(latent, first) + product(incoming, second)).astype(jnp.bfloat16)
    return (latent.astype(jnp.float32) + normed(product(hidden, third))).astype(jnp.bfloat16)


def coarse_update(latent, incoming, coarse_w1, coarse_w2, coarse_w3, w_descend):
    updated = node_update(latent, incoming.astype(jnp.bfloat16), coarse_w1, coarse_w2, coarse_w3)
    return (updated, product(updated, w_descend).astype(jnp.bfloat16))


def selector_rows(row_ids, width):
    columns = lax.broadcasted_iota(jnp.int32, (row_ids.shape[0], width), 1)
    return (columns == row_ids[:, None]).astype(jnp.bfloat16)


def edge_update(
    node_table, lifted, source, target, edge_w_src, edge_w_dst, edge_w2, node_w1, node_w2, node_w3
):
    fine_count = lifted.shape[0]
    sender = product(node_table, edge_w_src).astype(jnp.bfloat16)
    receiver = product(lifted, edge_w_dst).astype(jnp.bfloat16)
    source_pick = selector_rows(source, node_table.shape[0])
    target_pick = selector_rows(target, fine_count)
    edge_sum = product(source_pick, sender) + product(target_pick, receiver)
    edge_hidden = jax.nn.silu(edge_sum).astype(jnp.bfloat16)
    hidden_sums = lax.dot_general(
        target_pick, edge_hidden, (((0,), (0,)), ((), ())), preferred_element_type=jnp.float32
    )
    aggregate = jnp.dot(hidden_sums, edge_w2.astype(jnp.float32), precision=lax.Precision.HIGHEST)
    return node_update(lifted, aggregate.astype(jnp.bfloat16), node_w1, node_w2, node_w3)


def on_device(
    fine_latent,
    mid_latent,
    coarse_latent,
    fine_parent,
    mid_parent,
    halo_rows,
    edge_source,
    edge_target,
    w_child,
    mid_w1,
    mid_w2,
    mid_w3,
    w_coarse,
    coarse_w1,
    coarse_w2,
    coarse_w3,
    w_descend,
    w_fine,
    edge_w_src,
    edge_w_dst,
    edge_w2,
    node_w1,
    node_w2,
    node_w3,
):
    fine_count = fine_latent.shape[0]
    mid_count = mid_latent.shape[0]
    coarse_count = coarse_latent.shape[0]
    rim_count = halo_rows.shape[0] // 2
    child_msg = product(fine_latent, w_child).astype(jnp.bfloat16)
    slot_ids = lax.broadcasted_iota(jnp.int32, (3 * mid_count, fine_count), 0)
    picker = (slot_ids == fine_parent[None, :]).astype(jnp.bfloat16)
    partial_sums = product(picker, child_msg)
    extended = extended_2(partial_sums[mid_count:], (("tile", 0),), mid_count)
    mid_in = partial_sums[:mid_count] + extended[:mid_count] + extended[3 * mid_count :]
    mid_up = node_update(mid_latent, mid_in.astype(jnp.bfloat16), mid_w1, mid_w2, mid_w3)
    mid_msg = product(mid_up, w_coarse).astype(jnp.bfloat16)
    coarse_ids = lax.broadcasted_iota(jnp.int32, (coarse_count, mid_count), 0)
    selector = (coarse_ids == mid_parent[None, :]).astype(jnp.bfloat16)
    coarse_in = lax.psum(product(selector, mid_msg), ("rhombus", "tile"))
    coarse_out, down_coarse = coarse_update(
        coarse_latent, coarse_in, coarse_w1, coarse_w2, coarse_w3, w_descend
    )
    lookup = selector_rows(mid_parent, coarse_count)
    mid_out = (mid_up.astype(jnp.float32) + product(lookup, down_coarse)).astype(jnp.bfloat16)
    fine_down = product(mid_out, w_fine).astype(jnp.bfloat16)
    nearby = extended_2(fine_down, (("tile", 0),), mid_count)
    remapped = jnp.where(
        fine_parent < mid_count,
        fine_parent + mid_count,
        jnp.where(fine_parent < 2 * mid_count, fine_parent - mid_count, fine_parent),
    )
    parent_pick = selector_rows(remapped, 3 * mid_count)
    lifted = (fine_latent.astype(jnp.float32) + product(parent_pick, nearby)).astype(jnp.bfloat16)
    boundary = product(selector_rows(halo_rows, fine_count), lifted).astype(jnp.bfloat16)
    bordered = extended_2(boundary, (("tile", 0),), rim_count)
    node_table = jnp.concatenate([lifted, bordered[:rim_count], bordered[3 * rim_count :]], axis=0)
    fine_out = edge_update(
        node_table,
        lifted,
        edge_source,
        edge_target,
        edge_w_src,
        edge_w_dst,
        edge_w2,
        node_w1,
        node_w2,
        node_w3,
    )
    return (fine_out, mid_out, coarse_out)


def solution(mesh):
    placed = (
        P(("rhombus", "tile"), None),
        P(("rhombus", "tile"), None),
        P(),
        P(("rhombus", "tile")),
        P(("rhombus", "tile")),
        P(("rhombus", "tile")),
        P(("rhombus", "tile")),
        P(("rhombus", "tile")),
        P(),
        P(),
        P(),
        P(),
        P(),
        P(),
        P(),
        P(),
        P(),
        P(),
        P(),
        P(),
        P(),
        P(),
        P(),
        P(),
    )
    return jax.shard_map(
        on_device,
        mesh=mesh,
        in_specs=placed,
        out_specs=(P(("rhombus", "tile"), None), P(("rhombus", "tile"), None), P()),
        check_vma=False,
    )
```

profile of v0, /device:TPU:11, one launch (start us, length us, event | category | flops | bytes accessed | tf_op | source)
XLA Modules:
  0.0 110.9 jit_solution(14659364361576790947)
XLA Ops:
  0.6 0.0 copy-start
  0.7 1.9 %fusion.9 = f32[96,512]{1,0:T(8,128)S(1)} fusion(bf16[512,512]{1,0:T(8,128)(2,1)} %param.24, bf16[512,512]{1,0:T(8,128)(2,1)} %param.32, s32[512]{0:T(512)} %param.27), kind=kOutput, calls=%fused_computation.23 | convolution fusion | flops 319078400 | bytes 1247232 | tf_op jit(solution)/shard_map/dot_general | solution.py:23
  2.7 3.8 %collective-permute-start = (f32[32,512]{1,0:T(8,128)S(1)}, f32[32,512]{1,0:T(8,128)S(1)}, u32[]{:S(2)}, u32[]{:S(2)}) collective-permute-start(f32[32,512]{1,0:T(8,128)S(1)} %get-tuple-element.5), channel_id=1, source_target_pairs={{0,1},{1,2},{2,3},{3,4},{4,5},{5,6},{6,7},{8,9},{9,10},{10,11},{11... | collective-permute-start | bytes 196616 | tf_op jit(solution)/shard_map/ppermute | solution.py:16
  6.5 1.9 %collective-permute-start.1 = (f32[32,512]{1,0:T(8,128)S(1)}, f32[32,512]{1,0:T(8,128)S(1)}, u32[]{:S(2)}, u32[]{:S(2)}) collective-permute-start(f32[32,512]{1,0:T(8,128)S(1)} %get-tuple-element.6), channel_id=1, source_target_pairs={{1,0},{2,1},{3,2},{4,3},{5,4},{6,5},{7,6},{9,8},{10,9},{11,10},{12... | collective-permute-start | bytes 196616 | tf_op jit(solution)/shard_map/ppermute | solution.py:17
  8.4 1.6 %fusion.51 = f32[642,512]{1,0:T(8,128)} fusion(bf16[642,512]{1,0:T(8,128)(2,1)S(1)} %copy-done.1, bf16[512,512]{1,0:T(8,128)(2,1)S(1)} %copy-done.3), kind=kOutput, calls=%fused_computation.80 | convolution fusion | flops 336592896 | bytes 2496512 | tf_op jit(solution)/shard_map/dot_general | solution.py:23
  10.0 0.2 fusion.50
  10.2 2.7 %collective-permute-done.1 = f32[32,512]{1,0:T(8,128)S(1)} collective-permute-done((f32[32,512]{1,0:T(8,128)S(1)}, f32[32,512]{1,0:T(8,128)S(1)}, u32[]{:S(2)}, u32[]{:S(2)}) %collective-permute-start.1) | collective-permute-done | bytes 65568 | tf_op jit(solution)/shard_map/ppermute | solution.py:17
  13.0 0.5 multiply_reduce_fusion.2
  13.5 0.1 add_convert_fusion.2
  13.6 0.5 fusion.12
  14.1 51.6 %all-reduce.1 = bf16[642,512]{1,0:T(8,128)(2,1)S(1)} all-reduce(f32[642,512]{1,0:T(8,128)S(1)} %fusion.12), channel_id=1, replica_groups=mesh['rhombus'=4,'tile'=8] {'rhombus','tile'}, use_global_device_ids=true, to_apply=%region_1.2 | all-reduce | flops 328704 | bytes 1972224 | tf_op jit(solution)/shard_map/psum | solution.py:102
  65.7 2.8 %multiply_reduce_fusion = (f32[642]{0:T(1024)S(1)}, f32[642,512]{1,0:T(8,128)S(1)}) fusion(bf16[512,512]{1,0:T(8,128)(2,1)} %param.39, f32[642,512]{1,0:T(8,128)} %fusion.51, bf16[512,512]{1,0:T(8,128)(2,1)} %param.38, bf16[642,512]{1,0:T(8,128)(2,1)S(1)} %all-reduce.1), kind=kOutput, calls=%fused_computation.15 | convolution fusion | flops 675814784 | bytes 4338184 | tf_op jit(solution)/shard_map/dot_general | solution.py:23
  68.4 0.3 add_convert_fusion
  68.7 0.0 copy-start.2
  68.8 2.0 %fusion.11 = bf16[32,512]{1,0:T(8,128)(2,1)S(1)} fusion(bf16[642,512]{1,0:T(8,128)(2,1)S(1)} %add_convert_fusion, bf16[512,512]{1,0:T(8,128)(2,1)} %param.40, bf16[32,512]{1,0:T(8,128)(2,1)S(1)} %add_convert_fusion.2, s32[32]{0:T(128)S(1)} %copy-done.14), kind=kOutput, calls=%fused_computation.27 | convolution fusion | flops 358028352 | bytes 1247360 | tf_op jit(solution)/shard_map/dot_general | solution.py:23
  70.8 0.2 convolution_convert_fusion.6
  71.0 5.2 %collective-permute-start.2 = (bf16[32,512]{1,0:T(8,128)(2,1)S(1)}, bf16[32,512]{1,0:T(8,128)(2,1)S(1)}, u32[]{:S(2)}, u32[]{:S(2)}) collective-permute-start(bf16[32,512]{1,0:T(8,128)(2,1)S(1)} %convolution_convert_fusion.6), channel_id=1, source_target_pairs={{0,1},{1,2},{2,3},{3,4},{4,5},{5,6},{6,7},{8,9},{9,10},{10,11},{11... | collective-permute-start | bytes 98312 | tf_op jit(solution)/shard_map/ppermute | solution.py:16
  76.2 1.9 %collective-permute-start.3 = (bf16[32,512]{1,0:T(8,128)(2,1)S(1)}, bf16[32,512]{1,0:T(8,128)(2,1)S(1)}, u32[]{:S(2)}, u32[]{:S(2)}) collective-permute-start(bf16[32,512]{1,0:T(8,128)(2,1)S(1)} %convolution_convert_fusion.6), channel_id=1, source_target_pairs={{1,0},{2,1},{3,2},{4,3},{5,4},{6,5},{7,6},{9,8},{10,9},{11,10},{12... | collective-permute-start | bytes 98312 | tf_op jit(solution)/shard_map/ppermute | solution.py:17
  78.1 4.2 %collective-permute-done.3 = bf16[32,512]{1,0:T(8,128)(2,1)S(1)} collective-permute-done((bf16[32,512]{1,0:T(8,128)(2,1)S(1)}, bf16[32,512]{1,0:T(8,128)(2,1)S(1)}, u32[]{:S(2)}, u32[]{:S(2)}) %collective-permute-start.3) | collective-permute-done | bytes 32800 | tf_op jit(solution)/shard_map/ppermute | solution.py:17
  82.3 0.4 fusion.6
  82.7 0.3 convolution_convert_fusion.5
  83.1 1.9 %collective-permute-start.4 = (bf16[128,512]{1,0:T(8,128)(2,1)S(1)}, bf16[128,512]{1,0:T(8,128)(2,1)}, u32[]{:S(2)}, u32[]{:S(2)}) collective-permute-start(bf16[128,512]{1,0:T(8,128)(2,1)S(1)} %get-tuple-element.3), channel_id=1, source_target_pairs={{0,1},{1,2},{2,3},{3,4},{4,5},{5,6},{6,7},{8,9},{9,10},{10,11},{11... | collective-permute-start | bytes 393224 | tf_op jit(solution)/shard_map/ppermute | solution.py:16
  85.0 2.7 %collective-permute-start.5 = (bf16[128,512]{1,0:T(8,128)(2,1)S(1)}, bf16[128,512]{1,0:T(8,128)(2,1)}, u32[]{:S(2)}, u32[]{:S(2)}) collective-permute-start(bf16[128,512]{1,0:T(8,128)(2,1)S(1)} %get-tuple-element.4), channel_id=1, source_target_pairs={{1,0},{2,1},{3,2},{4,3},{5,4},{6,5},{7,6},{9,8},{10,9},{11,10},{12... | collective-permute-start | bytes 393224 | tf_op jit(solution)/shard_map/ppermute | solution.py:17
  87.7 4.8 %fusion.2 = f32[3072,512]{1,0:T(8,128)} fusion(s32[3072]{0:T(1024)S(1)} %copy-done.16, bf16[512,512]{1,0:T(8,128)(2,1)S(1)} %fusion.6, bf16[512,512]{1,0:T(8,128)(2,1)S(1)} %copy-done), kind=kOutput, calls=%fused_computation.5 | convolution fusion | flops 1880883200 | bytes 7352320 | tf_op jit(solution)/shard_map/dot_general | solution.py:23
  92.5 0.4 fusion.52
  93.0 0.6 copy-done.15
  93.6 2.4 %convolution_convert_fusion = bf16[768,512]{1,0:T(8,128)(2,1)} fusion(bf16[512,512]{1,0:T(8,128)(2,1)S(1)} %copy-done.15, bf16[128,512]{1,0:T(8,128)(2,1)} %collective-permute-done.5, bf16[128,512]{1,0:T(8,128)(2,1)} %collective-permute-done.4, bf16[512,512]{1,0:T(8,128)(2,1)S(1)} %fusion.6), kind=kOutput, calls=%fused_computation.10 | convolution fusion | flops 405405696 | bytes 2097152 | tf_op jit(solution)/shard_map/dot_general | solution.py:23
  96.0 8.3 %fusion.1 = f32[512,512]{1,0:T(8,128)S(1)} fusion(s32[3072]{0:T(1024)S(1)} %copy-done.16, f32[3072,512]{1,0:T(8,128)} %fusion.2, bf16[768,512]{1,0:T(8,128)(2,1)} %convolution_convert_fusion, s32[3072]{0:T(1024)S(1)} %copy-done.17), kind=kOutput, calls=%fused_computation.4 | convolution fusion | flops 4039901184 | bytes 8151040 | tf_op jit(solution)/shard_map/dot_general | solution.py:55
  104.3 2.8 %convolution_convert_fusion.4 = bf16[512,512]{1,0:T(8,128)(2,1)} fusion(f32[512,512]{1,0:T(8,128)S(1)} %fusion.1, bf16[512,512]{1,0:T(8,128)(2,1)} %param.44), kind=kOutput, calls=%fused_computation.20 | convolution fusion | flops 1610874880 | bytes 2097152 | tf_op jit(solution)/shard_map/dot_general | solution.py:58
  107.2 2.4 %multiply_reduce_fusion.1 = (f32[512]{0:T(512)S(1)}, f32[512,512]{0,1:T(8,128)S(1)}) fusion(bf16[512,512]{1,0:T(8,128)(2,1)} %param.47, f32[512,512]{1,0:T(8,128)S(1)} %fusion.52, bf16[512,512]{1,0:T(8,128)(2,1)} %convolution_convert_fusion.4, bf16[512,512]{1,0:T(8,128)(2,1)} %param.46), kind=kOutput, calls=%fused_computation.32 | convolution fusion | flops 538967552 | bytes 3672064 | tf_op jit(solution)/shard_map/dot_general | solution.py:23
  109.5 0.3 copy.27
  109.9 1.0 add_convert_fusion.1
  (45 shorter events, 0.2 us)
Async XLA Ops:
  0.6 87.1 %copy-start = (bf16[512,512]{1,0:T(8,128)(2,1)S(1)}, bf16[512,512]{1,0:T(8,128)(2,1)}, u32[]{:S(2)}) copy-start(bf16[512,512]{1,0:T(8,128)(2,1)} %param.43) | copy-start | bytes 1572868
  0.6 7.8 %copy-start.1 = (bf16[642,512]{1,0:T(8,128)(2,1)S(1)}, bf16[642,512]{1,0:T(8,128)(2,1)}, u32[]{:S(2)}) copy-start(bf16[642,512]{1,0:T(8,128)(2,1)} %param.26) | copy-start | bytes 1972228
  0.7 7.8 %copy-start.3 = (bf16[512,512]{1,0:T(8,128)(2,1)S(1)}, bf16[512,512]{1,0:T(8,128)(2,1)}, u32[]{:S(2)}) copy-start(bf16[512,512]{1,0:T(8,128)(2,1)} %param.37) | copy-start | bytes 1572868
  2.6 7.4 %copy-start.6 = (bf16[512,512]{1,0:T(8,128)(2,1)S(1)}, bf16[512,512]{1,0:T(8,128)(2,1)}, u32[]{:S(2)}) copy-start(bf16[512,512]{1,0:T(8,128)(2,1)} %param.33) | copy-start | bytes 1572868
  2.6 7.4 %copy-start.11 = (bf16[32,512]{1,0:T(8,128)(2,1)S(1)}, bf16[32,512]{1,0:T(8,128)(2,1)}, u32[]{:S(2)}) copy-start(bf16[32,512]{1,0:T(8,128)(2,1)} %param.25) | copy-start | bytes 98308
  2.6 10.3 %copy-start.4 = (bf16[512,512]{1,0:T(8,128)(2,1)S(1)}, bf16[512,512]{1,0:T(8,128)(2,1)}, u32[]{:S(2)}) copy-start(bf16[512,512]{1,0:T(8,128)(2,1)} %param.35) | copy-start | bytes 1572868
  2.7 10.3 %copy-start.5 = (bf16[512,512]{1,0:T(8,128)(2,1)S(1)}, bf16[512,512]{1,0:T(8,128)(2,1)}, u32[]{:S(2)}) copy-start(bf16[512,512]{1,0:T(8,128)(2,1)} %param.34) | copy-start | bytes 1572868
  2.7 7.6 %collective-permute-start = (f32[32,512]{1,0:T(8,128)S(1)}, f32[32,512]{1,0:T(8,128)S(1)}, u32[]{:S(2)}, u32[]{:S(2)}) collective-permute-start(f32[32,512]{1,0:T(8,128)S(1)} %get-tuple-element.5), channel_id=1, source_target_pairs={{0,1},{1,2},{2,3},{3,4},{4,5},{5,6},{6,7},{8,9},{9,10},{10,11},{11... | collective-permute-start | bytes 196616 | tf_op jit(solution)/shard_map/ppermute | solution.py:16
  6.5 6.5 %collective-permute-start.1 = (f32[32,512]{1,0:T(8,128)S(1)}, f32[32,512]{1,0:T(8,128)S(1)}, u32[]{:S(2)}, u32[]{:S(2)}) collective-permute-start(f32[32,512]{1,0:T(8,128)S(1)} %get-tuple-element.6), channel_id=1, source_target_pairs={{1,0},{2,1},{3,2},{4,3},{5,4},{6,5},{7,6},{9,8},{10,9},{11,10},{12... | collective-permute-start | bytes 196616 | tf_op jit(solution)/shard_map/ppermute | solution.py:17
  10.0 3.5 %copy-start.9 = (bf16[512,512]{1,0:T(8,128)(2,1)S(1)}, bf16[512,512]{1,0:T(8,128)(2,1)}, u32[]{:S(2)}) copy-start(bf16[512,512]{1,0:T(8,128)(2,1)} %param.36) | copy-start | bytes 1572868
  10.0 3.5 %copy-start.14 = (s32[32]{0:T(128)S(1)}, s32[32]{0:T(128)}, u32[]{:S(2)}) copy-start(s32[32]{0:T(128)} %param.28) | copy-start | bytes 388
  68.7 14.0 %copy-start.2 = (bf16[642,512]{1,0:T(8,128)(2,1)}, bf16[642,512]{1,0:T(8,128)(2,1)S(1)}, u32[]{:S(2)}) copy-start(bf16[642,512]{1,0:T(8,128)(2,1)S(1)} %add_convert_fusion) | copy-start | bytes 1972228
  68.7 2.0 %copy-start.7 = (bf16[512,512]{1,0:T(8,128)(2,1)S(1)}, bf16[512,512]{1,0:T(8,128)(2,1)}, u32[]{:S(2)}) copy-start(bf16[512,512]{1,0:T(8,128)(2,1)} %param.41) | copy-start | bytes 1572868
  68.7 9.4 %copy-start.13 = (s32[512]{0:T(512)S(1)}, s32[512]{0:T(512)}, u32[]{:S(2)}) copy-start(s32[512]{0:T(512)} %param.27) | copy-start | bytes 6148
  68.7 13.6 %copy-start.8 = (bf16[512,512]{1,0:T(8,128)(2,1)S(1)}, bf16[512,512]{1,0:T(8,128)(2,1)}, u32[]{:S(2)}) copy-start(bf16[512,512]{1,0:T(8,128)(2,1)} %param.24) | copy-start | bytes 1572868
  68.8 13.9 %copy-start.18 = (s32[256]{0:T(256)S(1)}, s32[256]{0:T(256)}, u32[]{:S(2)}) copy-start(s32[256]{0:T(256)} %param.29) | copy-start | bytes 3076
  70.7 21.8 %copy-start.12 = (bf16[32,512]{1,0:T(8,128)(2,1)}, bf16[32,512]{1,0:T(8,128)(2,1)S(1)}, u32[]{:S(2)}) copy-start(bf16[32,512]{1,0:T(8,128)(2,1)S(1)} %fusion.11) | copy-start | bytes 98308
  70.8 17.0 %copy-start.16 = (s32[3072]{0:T(1024)S(1)}, s32[3072]{0:T(1024)}, u32[]{:S(2)}) copy-start(s32[3072]{0:T(1024)} %param.31) | copy-start | bytes 36868
  71.0 7.2 %collective-permute-start.2 = (bf16[32,512]{1,0:T(8,128)(2,1)S(1)}, bf16[32,512]{1,0:T(8,128)(2,1)S(1)}, u32[]{:S(2)}, u32[]{:S(2)}) collective-permute-start(bf16[32,512]{1,0:T(8,128)(2,1)S(1)} %convolution_convert_fusion.6), channel_id=1, source_target_pairs={{0,1},{1,2},{2,3},{3,4},{4,5},{5,6},{6,7},{8,9},{9,10},{10,11},{11... | collective-permute-start | bytes 98312 | tf_op jit(solution)/shard_map/ppermute | solution.py:16
  76.2 6.1 %collective-permute-start.3 = (bf16[32,512]{1,0:T(8,128)(2,1)S(1)}, bf16[32,512]{1,0:T(8,128)(2,1)S(1)}, u32[]{:S(2)}, u32[]{:S(2)}) collective-permute-start(bf16[32,512]{1,0:T(8,128)(2,1)S(1)} %convolution_convert_fusion.6), channel_id=1, source_target_pairs={{1,0},{2,1},{3,2},{4,3},{5,4},{6,5},{7,6},{9,8},{10,9},{11,10},{12... | collective-permute-start | bytes 98312 | tf_op jit(solution)/shard_map/ppermute | solution.py:17
  83.1 9.9 %collective-permute-start.4 = (bf16[128,512]{1,0:T(8,128)(2,1)S(1)}, bf16[128,512]{1,0:T(8,128)(2,1)}, u32[]{:S(2)}, u32[]{:S(2)}) collective-permute-start(bf16[128,512]{1,0:T(8,128)(2,1)S(1)} %get-tuple-element.3), channel_id=1, source_target_pairs={{0,1},{1,2},{2,3},{3,4},{4,5},{5,6},{6,7},{8,9},{9,10},{10,11},{11... | collective-permute-start | bytes 393224 | tf_op jit(solution)/shard_map/ppermute | solution.py:16
  85.0 7.6 %copy-start.10 = (bf16[512,512]{1,0:T(8,128)(2,1)S(1)}, bf16[512,512]{1,0:T(8,128)(2,1)}, u32[]{:S(2)}) copy-start(bf16[512,512]{1,0:T(8,128)(2,1)} %param.45) | copy-start | bytes 1572868
  85.0 8.0 %collective-permute-start.5 = (bf16[128,512]{1,0:T(8,128)(2,1)S(1)}, bf16[128,512]{1,0:T(8,128)(2,1)}, u32[]{:S(2)}, u32[]{:S(2)}) collective-permute-start(bf16[128,512]{1,0:T(8,128)(2,1)S(1)} %get-tuple-element.4), channel_id=1, source_target_pairs={{1,0},{2,1},{3,2},{4,3},{5,4},{6,5},{7,6},{9,8},{10,9},{11,10},{12... | collective-permute-start | bytes 393224 | tf_op jit(solution)/shard_map/ppermute | solution.py:17
  92.5 1.0 copy-start.15
  93.0 3.1 %copy-start.17 = (s32[3072]{0:T(1024)S(1)}, s32[3072]{0:T(1024)}, u32[]{:S(2)}) copy-start(s32[3072]{0:T(1024)} %param.30) | copy-start | bytes 36868
where the time goes:
time: 113 us; the launch traced here: 111 us
  blocking collectives  51.6 us (46%)
  matrix products  31.5 us (28%)
  starting transfers between devices  17.5 us (15%)
  waiting for transfers between devices  6.91 us (6%)
  other arithmetic  1.4 us (1%)
    psum x1, blocking collectives, on_device(): coarse_in = lax.psum(product(selector, mid_msg), ('rhombus', 'tile'))  51.6 us
    dot_general x14, matrix products, product(): return jnp.dot(left, right, preferred_element_type=jnp.float32)  20.4 us
    ppermute x3, starting transfers between devices, extended_2(): before = lax.ppermute(last, axis, up)  10.9 us
    dot_general x1, matrix products, edge_update(): lax.dot_general(target_pick, edge_hidden, (((0,), (0,)), ((), ())), prefe...  8.29 us
    ppermute x3, waiting for transfers between devices, extended_2(): after = lax.ppermute(leading, axis, down)  6.9 us
    ppermute x3, starting transfers between devices, extended_2(): after = lax.ppermute(leading, axis, down)  6.56 us
    dot_general x1, matrix products, edge_update(): jnp.dot(hidden_sums, edge_w2.astype(jnp.float32), precision=lax.Precision...  2.83 us
  transfers between devices with their start and end apart: 6, of which 2 were waited for; matrix products, arithmetic and copies ran while one was open for 6% of the time, Pallas kernels for 0%

commit v1 on v0

v1 whole, which is shorter than its diff:
```python
import jax
import jax.numpy as jnp
from jax import lax
from jax.experimental import pallas as pl
from jax.experimental.pallas import tpu as pltpu
from jax.sharding import PartitionSpec as P

MESH = pl.DeviceIdType.MESH

EPSILON = 1e-05


def product(left, right):
    return jnp.dot(left, right, preferred_element_type=jnp.float32)


def normed(values):
    return values / jnp.sqrt(jnp.mean(values * values, axis=-1, keepdims=True) + EPSILON)


def node_update(latent, incoming, first, second, third):
    hidden = jax.nn.silu(product(latent, first) + product(incoming, second)).astype(jnp.bfloat16)
    return (latent.astype(jnp.float32) + normed(product(hidden, third))).astype(jnp.bfloat16)


def selector_rows(row_ids, width):
    columns = lax.broadcasted_iota(jnp.int32, (row_ids.shape[0], width), 1)
    return (columns == row_ids[:, None]).astype(jnp.bfloat16)


def edge_update(
    node_table, lifted, source, target, edge_w_src, edge_w_dst, edge_w2, node_w1, node_w2, node_w3
):
    fine_count = lifted.shape[0]
    sender = product(node_table, edge_w_src).astype(jnp.bfloat16)
    receiver = product(lifted, edge_w_dst).astype(jnp.bfloat16)
    source_pick = selector_rows(source, node_table.shape[0])
    target_pick = selector_rows(target, fine_count)
    edge_sum = product(source_pick, sender) + product(target_pick, receiver)
    edge_hidden = jax.nn.silu(edge_sum).astype(jnp.bfloat16)
    hidden_sums = lax.dot_general(
        target_pick, edge_hidden, (((0,), (0,)), ((), ())), preferred_element_type=jnp.float32
    )
    leading = hidden_sums.astype(jnp.bfloat16)
    rest = (hidden_sums - leading.astype(jnp.float32)).astype(jnp.bfloat16)
    aggregate = product(leading, edge_w2) + product(rest, edge_w2)
    return node_update(lifted, aggregate.astype(jnp.bfloat16), node_w1, node_w2, node_w3)


def one_hot(ids, axis, shape):
    return jnp.where(lax.broadcasted_iota(jnp.int32, shape, axis) == ids, 1.0, 0.0).astype(jnp.bfloat16)


def as_columns(row, width):
    count = row.shape[1]
    column = jnp.transpose(jnp.broadcast_to(row, (128, count)))
    return jnp.concatenate([column] * (width // 128), axis=1)


def gather_kernel(
    groups,
    tiles,
    fine_ref,
    parent_ref,
    halo_ref,
    latent_ref,
    coarse_id_ref,
    child_ref,
    w1_ref,
    w2_ref,
    w3_ref,
    ups_ref,
    ids_ref,
    rim_ref,
    rim_parent_ref,
    fine_v,
    child_v,
    w1_v,
    w2_v,
    w3_v,
    sums_v,
    beside_v,
    picked_v,
    picked_parent_v,
    load_sem,
    near_send,
    near_recv,
    tree_send,
    block_recv,
    id_recv,
):
    group, tile = (lax.axis_index("rhombus"), lax.axis_index("tile"))
    pairs = tiles // 2
    pair, core = (tile // 2, tile % 2)
    mids = latent_ref.shape[0]
    rims = halo_ref.shape[1] // 2
    fines = fine_ref.shape[0]

    loads = [
        pltpu.make_async_copy(src, dst, load_sem.at[i])
        for i, (src, dst) in enumerate(
            [(fine_ref, fine_v), (child_ref, child_v), (w1_ref, w1_v), (w2_ref, w2_v), (w3_ref, w3_v)]
        )
    ]
    for load in loads:
        load.start()

    def at(group_id, pair_id, core_id):
        return (group_id, pair_id * 2 + core_id)

    columns = [at((group + k) % groups, pair, core) for k in range(1, groups)]
    if pairs == 4:
        across, along = (pair + 1 - 2 * (pair % 2), (pair + 2) % 4)
        corner = (across + 2) % 4
        level = [across, along]
    else:
        level = [(pair + k) % pairs for k in range(1, pairs)]
    row_peers = [at(group, other, core) for other in level]
    partner = at(group, pair, 1 - core)
    peers = columns + row_peers + [partner]

    barrier = pltpu.get_barrier_semaphore()
    for peer in peers:
        pl.semaphore_signal(barrier, inc=1, device_id=peer, device_id_type=MESH)

    @pl.when(tile > 0)
    def _():
        pl.semaphore_signal(barrier, inc=1, device_id=(group, tile - 1), device_id_type=MESH)

    @pl.when(tile < tiles - 1)
    def _():
        pl.semaphore_signal(barrier, inc=1, device_id=(group, tile + 1), device_id_type=MESH)

    me = group * tiles + tile
    ids_ref[me] = coarse_id_ref[...]
    loads[0].wait()
    fine = fine_v[...]
    parents = parent_ref[...]
    picker = one_hot(parents, 0, (3 * mids, fines))
    sums_v[...] = product(picker, fine)
    pl.semaphore_wait(barrier, len(peers) + 1 + (tile + tiles - 1) // tiles - (tile + 1) // tiles)

    def near(index, source, target, device):
        return pltpu.make_async_remote_copy(
            src_ref=source,
            dst_ref=target,
            send_sem=near_send.at[index],
            recv_sem=near_recv.at[index],
            device_id=device,
            device_id_type=MESH,
        )

    before, after = ((group, tile - 1), (group, tile + 1))
    to_before = [
        near(0, sums_v.at[pl.ds(mids, mids)], beside_v.at[0], before),
        near(1, picked_v.at[pl.ds(0, rims)], rim_ref.at[pl.ds(rims, rims)], before),
        near(2, picked_parent_v.at[0], rim_parent_ref.at[1], before),
    ]
    to_after = [
        near(3, sums_v.at[pl.ds(2 * mids, mids)], beside_v.at[1], after),
        near(4, picked_v.at[pl.ds(rims, rims)], rim_ref.at[pl.ds(0, rims)], after),
        near(5, picked_parent_v.at[1], rim_parent_ref.at[0], after),
    ]

    @pl.when(tile > 0)
    def _():
        to_before[0].start()

    @pl.when(tile < tiles - 1)
    def _():
        to_after[0].start()

    halo = halo_ref[...]
    picked_v[...] = product(one_hot(as_columns(halo, fines), 1, (2 * rims, fines)), fine).astype(jnp.bfloat16)
    side = parents // mids
    shift = jnp.where(side == 1, -1, jnp.where(side == 2, 1, 0))
    global_parents = (me + shift) * mids + parents % mids
    parent_column = jnp.transpose(jnp.broadcast_to(global_parents, (128, fines)))
    for half in range(2):
        hit = lax.broadcasted_iota(jnp.int32, (fines, rims), 0) == halo[:, half * rims : (half + 1) * rims]
        spread = jnp.concatenate([parent_column] * (rims // 128), axis=1)
        picked_parent_v[half] = jnp.sum(jnp.where(hit, spread, 0), axis=0, keepdims=True)

    @pl.when(tile > 0)
    def _():
        to_before[1].start()
        to_before[2].start()

    @pl.when(tile < tiles - 1)
    def _():
        to_after[1].start()
        to_after[2].start()

    for load in loads[1:]:
        load.wait()
    kept = product(latent_ref[...], w1_v[...])

    @pl.when(tile > 0)
    def _():
        to_after[0].wait_recv()

    @pl.when(tile == 0)
    def _():
        beside_v[1] = jnp.zeros_like(beside_v[1])
        rim_ref[pl.ds(0, rims)] = jnp.zeros((rims, rim_ref.shape[1]), rim_ref.dtype)
        rim_parent_ref[0] = jnp.full(rim_parent_ref.shape[1:], -1, jnp.int32)

    @pl.when(tile < tiles - 1)
    def _():
        to_before[0].wait_recv()

    @pl.when(tile == tiles - 1)
    def _():
        beside_v[0] = jnp.zeros_like(beside_v[0])
        rim_ref[pl.ds(rims, rims)] = jnp.zeros((rims, rim_ref.shape[1]), rim_ref.dtype)
        rim_parent_ref[1] = jnp.full(rim_parent_ref.shape[1:], -1, jnp.int32)

    total = sums_v[pl.ds(0, mids)] + beside_v[0] + beside_v[1]
    leading = total.astype(jnp.bfloat16)
    rest = (total - leading.astype(jnp.float32)).astype(jnp.bfloat16)
    mid_in = (product(leading, child_v[...]) + product(rest, child_v[...])).astype(jnp.bfloat16)
    hidden = jax.nn.silu(kept + product(mid_in, w2_v[...])).astype(jnp.bfloat16)
    mid_up = latent_ref[...].astype(jnp.float32) + normed(product(hidden, w3_v[...]))
    ups_ref[me] = mid_up.astype(jnp.bfloat16)

    started = []

    def copies(slot, index, device):
        return [
            pltpu.make_async_remote_copy(
                src_ref=held.at[slot],
                dst_ref=held.at[slot],
                send_sem=tree_send.at[kind, index],
                recv_sem=sems.at[slot],
                device_id=device,
                device_id_type=MESH,
            )
            for kind, (held, sems) in enumerate([(ups_ref, block_recv), (ids_ref, id_recv)])
        ]

    def send(slot, devices):
        for device in devices:
            for copy in copies(slot, len(started) // 2, device):
                copy.start()
                started.append(copy)

    def arrive(slot):
        for copy in copies(slot, 0, partner):
            copy.wait_recv()

    def slot_of(k, pair_id, core_id):
        return (group + k) % groups * tiles + pair_id * 2 + core_id

    order = [0] + sorted(range(1, groups), key=lambda k: min(k, groups - k))
    send(me, columns + row_peers + [partner])
    for k in order:
        if k > 0:
            slot = slot_of(k, pair, core)
            arrive(slot)
            send(slot, row_peers + [partner])
    for n, k in enumerate(order):
        for place, other in enumerate(level):
            slot = slot_of(k, other, core)
            arrive(slot)
            onward = [partner]
            if pairs == 4 and n % 2 == place:
                onward = [at(group, level[1 - place], core), partner]
            send(slot, onward)
    if pairs == 4:
        for k in order:
            slot = slot_of(k, corner, core)
            arrive(slot)
            send(slot, [partner])
    for k in order:
        for other in range(pairs):
            arrive(slot_of(k, other, 1 - core))

    @pl.when(tile > 0)
    def _():
        for copy in to_after[1:]:
            copy.wait_recv()
        for copy in to_before:
            copy.wait_send()

    @pl.when(tile < tiles - 1)
    def _():
        for copy in to_before[1:]:
            copy.wait_recv()
        for copy in to_after:
            copy.wait_send()

    for copy in started:
        copy.wait_send()


def gathered(fine_latent, mid_latent, fine_parent, mid_parent, halo_rows, w_child, mid_w1, mid_w2, mid_w3):
    groups, tiles = (lax.axis_size("rhombus"), lax.axis_size("tile"))
    devices = groups * tiles
    mids, features = mid_latent.shape
    halos = halo_rows.shape[0]
    rims = halos // 2
    width = -(-mids // 128) * 128
    coarse_ids = jnp.pad(mid_parent[None, :], ((0, 0), (0, width - mids)))
    pairs = tiles // 2
    level = 2 if pairs == 4 else pairs - 1
    sends = groups + level + (groups - 1) * (level + 1) + groups * level
    sends += 2 * groups if pairs == 4 else 0
    bf16, f32, i32 = (jnp.bfloat16, jnp.float32, jnp.int32)
    vmem = pl.BlockSpec(memory_space=pltpu.VMEM)
    hbm = pl.BlockSpec(memory_space=pl.ANY)
    square = pltpu.VMEM((features, features), bf16)
    return pl.pallas_call(
        lambda *refs: gather_kernel(groups, tiles, *refs),
        out_shape=(
            jax.ShapeDtypeStruct((devices, mids, features), bf16),
            jax.ShapeDtypeStruct((devices, 1, width), i32),
            jax.ShapeDtypeStruct((halos, features), bf16),
            jax.ShapeDtypeStruct((2, 1, rims), i32),
        ),
        in_specs=[hbm, vmem, vmem, vmem, vmem, hbm, hbm, hbm, hbm],
        out_specs=(vmem, vmem, vmem, vmem),
        scratch_shapes=[
            pltpu.VMEM(fine_latent.shape, bf16),
            square,
            square,
            square,
            square,
            pltpu.VMEM((3 * mids, features), f32),
            pltpu.VMEM((2, mids, features), f32),
            pltpu.VMEM((halos, features), bf16),
            pltpu.VMEM((2, 1, rims), i32),
            pltpu.SemaphoreType.DMA((5,)),
            pltpu.SemaphoreType.DMA((6,)),
            pltpu.SemaphoreType.DMA((6,)),
            pltpu.SemaphoreType.DMA((2, sends)),
            pltpu.SemaphoreType.DMA((devices,)),
            pltpu.SemaphoreType.DMA((devices,)),
        ],
        compiler_params=pltpu.CompilerParams(collective_id=0, has_side_effects=True),
        name="gather_mids",
    )(
        fine_latent,
        fine_parent[None, :],
        halo_rows[None, :],
        mid_latent,
        coarse_ids,
        w_child,
        mid_w1,
        mid_w2,
        mid_w3,
    )


def on_device(
    fine_latent,
    mid_latent,
    coarse_latent,
    fine_parent,
    mid_parent,
    halo_rows,
    edge_source,
    edge_target,
    w_child,
    mid_w1,
    mid_w2,
    mid_w3,
    w_coarse,
    coarse_w1,
    coarse_w2,
    coarse_w3,
    w_descend,
    w_fine,
    edge_w_src,
    edge_w_dst,
    edge_w2,
    node_w1,
    node_w2,
    node_w3,
):
    mid_count = mid_latent.shape[0]
    coarse_count = coarse_latent.shape[0]
    rim_count = halo_rows.shape[0] // 2
    tiles = lax.axis_size("tile")
    me = lax.axis_index("rhombus") * tiles + lax.axis_index("tile")
    ups, ids, rim, rim_parent = gathered(
        fine_latent, mid_latent, fine_parent, mid_parent, halo_rows, w_child, mid_w1, mid_w2, mid_w3
    )
    mid_all = ups.reshape(-1, ups.shape[-1])
    id_all = ids[:, 0, :mid_count].reshape(-1)
    mid_msg = product(mid_all, w_coarse).astype(jnp.bfloat16)
    coarse_ids = lax.broadcasted_iota(jnp.int32, (coarse_count, id_all.shape[0]), 0)
    selector = (coarse_ids == id_all[None, :]).astype(jnp.bfloat16)
    coarse_in = product(selector, mid_msg).astype(jnp.bfloat16)
    coarse_out = node_update(coarse_latent, coarse_in, coarse_w1, coarse_w2, coarse_w3)
    reach = min(5 * mid_count, id_all.shape[0])
    low = jnp.clip((me - 2) * mid_count, 0, id_all.shape[0] - reach)
    near_up = lax.dynamic_slice_in_dim(mid_all, low, reach, 0)
    near_id = lax.dynamic_slice_in_dim(id_all, low, reach, 0)
    picked = product(selector_rows(near_id, coarse_count), coarse_out).astype(jnp.bfloat16)
    down = product(picked, w_descend).astype(jnp.bfloat16)
    near_out = (near_up.astype(jnp.float32) + down.astype(jnp.float32)).astype(jnp.bfloat16)
    mid_out = lax.dynamic_slice_in_dim(near_out, me * mid_count - low, mid_count, 0)
    fine_down = product(near_out, w_fine).astype(jnp.bfloat16)
    side = fine_parent // mid_count
    shift = jnp.where(side == 1, -1, jnp.where(side == 2, 1, 0))
    own_parent = (me + shift) * mid_count + fine_parent % mid_count
    table_parent = jnp.concatenate([own_parent, rim_parent.reshape(-1)]) - low
    table_parent = jnp.where(
        jnp.concatenate([own_parent, rim_parent.reshape(-1)]) < 0, -1, table_parent
    )
    raised = product(selector_rows(table_parent, reach), fine_down)
    node_table = (jnp.concatenate([fine_latent, rim], axis=0).astype(jnp.float32) + raised).astype(jnp.bfloat16)
    lifted = node_table[: fine_latent.shape[0]]
    fine_out = edge_update(
        node_table,
        lifted,
        edge_source,
        edge_target,
        edge_w_src,
        edge_w_dst,
        edge_w2,
        node_w1,
        node_w2,
        node_w3,
    )
    return (fine_out, mid_out, coarse_out)


def solution(mesh):
    placed = (
        P(("rhombus", "tile"), None),
        P(("rhombus", "tile"), None),
        P(),
        P(("rhombus", "tile")),
        P(("rhombus", "tile")),
        P(("rhombus", "tile")),
        P(("rhombus", "tile")),
        P(("rhombus", "tile")),
        P(),
        P(),
        P(),
        P(),
        P(),
        P(),
        P(),
        P(),
        P(),
        P(),
        P(),
        P(),
        P(),
        P(),
        P(),
        P(),
    )
    return jax.shard_map(
        on_device,
        mesh=mesh,
        in_specs=placed,
        out_specs=(P(("rhombus", "tile"), None), P(("rhombus", "tile"), None), P()),
        check_vma=False,
    )
```

time: 113 us -> 64.3 us (0.57); the launches traced: 111 us -> 63.7 us
  blocking collectives: 51.6 us -> 0 us
  Pallas kernels: 0 us -> 23.8 us
  starting transfers between devices: 17.5 us -> 0 us
  waiting for transfers between devices: 6.91 us -> 0 us
  local copies, waits for them, and re-layouts: 1.04 us -> 4.11 us
  other arithmetic: 1.4 us -> 2.75 us
    psum x1 -> x0, blocking collectives: 51.6 us -> none  [on_device(): coarse_in = lax.psum(product(selector, mid_msg), ('rhombus', 'tile'))]
    pallas_call x0 -> x1, Pallas kernels: none -> 23.8 us  [gathered(): pl.pallas_call(lambda *refs: gather_kernel(groups, tiles, *refs), out_sha...]
    ppermute x6 -> x0, starting transfers between devices: 17.5 us -> none  [the longest x3 10.9 us: extended_2(): before = lax.ppermute(last, axis, up)]
    ppermute x6 -> x0, waiting for transfers between devices: 6.91 us -> none  [the longest x3 6.9 us: extended_2(): after = lax.ppermute(leading, axis, down)]
    dot_general x14 -> x11, matrix products: 20.4 us -> 24.1 us  [product(): return jnp.dot(left, right, preferred_element_type=jnp.float32)]
    dot_general x1 -> x0, matrix products: 2.83 us -> none  [edge_update(): jnp.dot(hidden_sums, edge_w2.astype(jnp.float32), precision=lax.Precision...]
    dynamic_slice x0 -> x2, local copies, waits for them, and re-layouts: none -> 1.48 us  [the longest x1 1.4 us: on_device(): lax.dynamic_slice_in_dim(near_out, me * mid_count - low, mid_count, 0)]
    convert_element_type x3 -> x2, other arithmetic: 1.37 us -> 2.71 us  [node_update(): (latent.astype(jnp.float32) + normed(product(hidden, third))).astype(jnp....]
  transfers between devices with their start and end apart: 6 -> 0, of which waited for: 2 -> 0; matrix products, arithmetic and copies ran while one was open for 6% -> 0% of each run, Pallas kernels for 0% -> 0%
where the time goes in v1:
time: 64.3 us; the launch traced here: 63.7 us
  matrix products  32.1 us (50%)
  Pallas kernels  23.8 us (37%)
  local copies, waits for them, and re-layouts  4.11 us (6%)
  other arithmetic  2.75 us (4%)
  between operations  0.88 us (1%)
    dot_general x11, matrix products, product(): return jnp.dot(left, right, preferred_element_type=jnp.float32)  24.1 us
    pallas_call x1, Pallas kernels, gathered(): pl.pallas_call(lambda *refs: gather_kernel(groups, tiles, *refs), out_sha...  23.8 us
    dot_general x1, matrix products, edge_update(): lax.dot_general(target_pick, edge_hidden, (((0,), (0,)), ((), ())), prefe...  8.04 us
    convert_element_type x2, other arithmetic, node_update(): (latent.astype(jnp.float32) + normed(product(hidden, third))).astype(jnp....  2.71 us
    dynamic_slice x1, local copies, waits for them, and re-layouts, on_device(): lax.dynamic_slice_in_dim(near_out, me * mid_count - low, mid_count, 0)  1.4 us

profile of v1, /device:TPU:11, one launch (start us, length us, event | category | flops | bytes accessed | tf_op | source)
XLA Modules:
  0.0 63.7 jit_solution(17938641539513938120)
XLA Ops:
  0.6 0.0 copy-start
  0.7 1.3 %pad.4.refs_4_ = s32[1,128]{1,0:T(1,128)} pad(s32[1,32]{1,0:T(1,128)} %bitcast.31, s32[]{:T(128)} %constant.29.clone.1), padding=0_0x0_96 | pad | bytes 644 | tf_op jit(solution)/shard_map/jit(_pad)/pad | solution.py:303
  1.9 23.8 %gather_mids.1 = (bf16[32,32,512]{2,1,0:T(8,128)(2,1)}, s32[32,1,128]{2,1,0:T(1,128)}, bf16[256,512]{1,0:T(8,128)(2,1)}, s32[2,1,128]{2,1,0:T(1,128)}) custom-call(bf16[512,512]{1,0:T(8,128)(2,1)} %refs_0_.1, s32[1,512]{1,0:T(1,128)} %bitcast.26, s32[1,256]{1,0:T(1,128)} %bitcast.27, bf16[32,512]{1,0:T(8,128)(2,1)} %refs_3_.1, s32[1,128]{1,0:T(1,128)} %pad.4.refs_4_, ...), custom_call_target="tpu_custom_call" | custom-call | tf_op jit(solution)/shard_map/gather_mids/pallas_call | solution.py:312
  25.7 0.8 %slice_reduce_fusion = s32[32,32]{1,0:T(8,128)S(1)} fusion(s32[32,1,128]{2,1,0:T(1,128)} %get-tuple-element.10), kind=kLoop, calls=%fused_computation.46 | loop fusion | bytes 8192 | tf_op jit(solution)/shard_map/slice | solution.py:389
  26.5 0.1 reshape_squeeze.3
  26.6 3.5 %fusion.7 = bf16[642,512]{1,0:T(8,128)(2,1)} fusion(s32[1024]{0:T(1024)S(1)} %reshape_squeeze.3, bf16[1024,512]{1,0:T(8,128)(2,1)} %bitcast.29, bf16[512,512]{1,0:T(8,128)(2,1)S(1)} %copy-done.9), kind=kOutput, calls=%fused_computation.17 | convolution fusion | flops 1211567104 | bytes 2234368 | tf_op jit(solution)/shard_map/dot_general | solution.py:14
  30.1 0.5 fusion.30
  30.7 3.5 %multiply_reduce_fusion = (f32[642]{0:T(1024)S(1)}, f32[642,512]{1,0:T(8,128)}) fusion(bf16[512,512]{1,0:T(8,128)(2,1)} %param.39, f32[642,512]{1,0:T(8,128)S(1)} %fusion.30, bf16[642,512]{1,0:T(8,128)(2,1)} %fusion.7, bf16[512,512]{1,0:T(8,128)(2,1)} %param.38), kind=kOutput, calls=%fused_computation.19 | convolution fusion | flops 675814784 | bytes 4338184 | tf_op jit(solution)/shard_map/dot_general | solution.py:14
  34.2 0.0 copy-start.6
  34.2 0.0 copy-start.4
  34.2 0.0 copy-start.12
  34.3 1.7 %add_convert_fusion.1 = bf16[642,512]{1,0:T(8,128)(2,1)S(1)} fusion(f32[642,512]{1,0:T(8,128)} %get-tuple-element.12, bf16[642,512]{1,0:T(8,128)(2,1)S(1)} %copy-done.1, f32[642]{0:T(1024)S(1)} %add_sqrt_fusion), kind=kLoop, calls=%fused_computation.18 | loop fusion | flops 1314816 | bytes 2632200 | tf_op jit(solution)/shard_map/convert_element_type | solution.py:23
  36.0 0.0 copy-start.2
  36.0 0.1 dynamic_slice.10
  36.1 1.6 %fusion.13 = bf16[160,512]{1,0:T(8,128)(2,1)S(1)} fusion(bf16[512,512]{1,0:T(8,128)(2,1)S(1)} %copy-done.10, bf16[642,512]{1,0:T(8,128)(2,1)S(1)} %add_convert_fusion.1, s32[160]{0:T(256)S(1)} %dynamic_slice.10, bf16[1024,512]{1,0:T(8,128)(2,1)} %bitcast.30, s32[]{:T(128)S(6)} %min.4), kind=kOutput, calls=%fused_computation.29 | convolution fusion | flops 189665600 | bytes 1510020 | tf_op jit(solution)/shard_map/dot_general | solution.py:14
  37.7 0.0 copy-start.13
  37.8 1.7 %add_convert_fusion = bf16[768,512]{1,0:T(8,128)(2,1)S(1)} fusion(bf16[160,512]{1,0:T(8,128)(2,1)S(1)} %fusion.13, bf16[512,512]{1,0:T(8,128)(2,1)} %param.41, bf16[256,512]{1,0:T(8,128)(2,1)S(1)} %copy-done.12, bf16[512,512]{1,0:T(8,128)(2,1)S(1)} %copy-done.4, s32[768]{0:T(1024)S(1)} %subtract_select_fusion), kind=kOutput, calls=%fused_computation.11 | convolution fusion | flops 212279296 | bytes 2264064 | tf_op jit(solution)/shard_map/dot_general | solution.py:14
  39.4 0.0 copy-done
  39.4 0.0 copy-done.13
  39.5 0.0 copy-start.11
  39.5 4.8 %fusion.2 = f32[3072,512]{1,0:T(8,128)} fusion(s32[3072]{0:T(1024)S(1)} %copy-done.13, bf16[512,512]{1,0:T(8,128)(2,1)S(1)} %copy-done, bf16[768,512]{1,0:T(8,128)(2,1)S(1)} %add_convert_fusion), kind=kOutput, calls=%fused_computation.5 | convolution fusion | flops 1880883200 | bytes 7352320 | tf_op jit(solution)/shard_map/dot_general | solution.py:14
  44.3 0.6 convolution_convert_fusion.1
  44.9 0.1 copy-done.14
  45.0 8.0 %fusion.1 = f32[512,512]{1,0:T(8,128)S(1)} fusion(s32[3072]{0:T(1024)S(1)} %copy-done.13, f32[3072,512]{1,0:T(8,128)} %fusion.2, bf16[768,512]{1,0:T(8,128)(2,1)S(1)} %convolution_convert_fusion.1, s32[3072]{0:T(1024)S(1)} %copy-done.14), kind=kOutput, calls=%fused_computation.4 | convolution fusion | flops 4039901184 | bytes 8151040 | tf_op jit(solution)/shard_map/dot_general | solution.py:41
  53.0 0.0 copy-start.5
  53.0 1.5 %fusion.22 = f32[512,512]{1,0:T(8,128)S(1)} fusion(bf16[512,512]{1,0:T(8,128)(2,1)} %param.44, f32[512,512]{1,0:T(8,128)S(1)} %fusion.1), kind=kOutput, calls=%fused_computation.43 | convolution fusion | flops 268697600 | bytes 2621440 | tf_op jit(solution)/shard_map/dot_general | solution.py:14
  54.6 1.4 %fusion.17 = f32[512,512]{1,0:T(8,128)} fusion(bf16[512,512]{1,0:T(8,128)(2,1)S(1)} %copy-done.5, bf16[768,512]{1,0:T(8,128)(2,1)S(1)} %add_convert_fusion), kind=kOutput, calls=%fused_computation.39 | convolution fusion | flops 268435456 | bytes 2097152 | tf_op jit(solution)/shard_map/dot_general | solution.py:14
  56.0 3.2 %multiply_convert_fusion.3 = bf16[512,512]{1,0:T(8,128)(2,1)} fusion(f32[512,512]{1,0:T(8,128)} %fusion.17, bf16[512,512]{1,0:T(8,128)(2,1)} %param.46, f32[512,512]{1,0:T(8,128)S(1)} %fusion.22, bf16[512,512]{1,0:T(8,128)(2,1)} %param.44, f32[512,512]{1,0:T(8,128)S(1)} %fusion.1), kind=kOutput, calls=%fused_computation.33 | convolution fusion | flops 540016640 | bytes 4718592 | tf_op jit(solution)/shard_map/dot_general | solution.py:14
  59.2 1.7 %multiply_reduce_fusion.1 = (f32[512]{0:T(512)S(1)}, f32[512,512]{0,1:T(8,128)S(1)}) fusion(bf16[512,512]{1,0:T(8,128)(2,1)} %multiply_convert_fusion.3, bf16[512,512]{1,0:T(8,128)(2,1)} %param.47), kind=kOutput, calls=%fused_computation.32 | convolution fusion | flops 268959232 | bytes 2099200 | tf_op jit(solution)/shard_map/dot_general | solution.py:14
  60.9 0.3 copy.27
  61.3 1.0 %add_convert_fusion.2 = bf16[512,512]{1,0:T(8,128)(2,1)} fusion(f32[512,512]{1,0:T(8,128)S(1)} %copy.27, f32[512]{0:T(512)S(1)} %add_sqrt_fusion.1, bf16[768,512]{1,0:T(8,128)(2,1)S(1)} %add_convert_fusion), kind=kLoop, calls=%fused_computation.31 | loop fusion | flops 1048576 | bytes 2099200 | tf_op jit(solution)/shard_map/convert_element_type | solution.py:23
  62.3 1.4 %constant_dynamic-slice_fusion = bf16[32,512]{1,0:T(8,128)(2,1)} fusion(bf16[160,512]{1,0:T(8,128)(2,1)} %copy-done.7, s32[]{:T(128)S(6)} %select_n.38), kind=kLoop, calls=%fused_computation.59 | loop fusion | bytes 65540 | tf_op jit(solution)/shard_map/dynamic_slice | solution.py:402
  (23 shorter events, 0.1 us)
Async XLA Ops:
  0.6 38.8 %copy-start = (bf16[512,512]{1,0:T(8,128)(2,1)S(1)}, bf16[512,512]{1,0:T(8,128)(2,1)}, u32[]{:S(2)}) copy-start(bf16[512,512]{1,0:T(8,128)(2,1)} %param.43) | copy-start | bytes 1572868
  0.6 25.9 %copy-start.9 = (bf16[512,512]{1,0:T(8,128)(2,1)S(1)}, bf16[512,512]{1,0:T(8,128)(2,1)}, u32[]{:S(2)}) copy-start(bf16[512,512]{1,0:T(8,128)(2,1)} %param.36) | copy-start | bytes 1572868
  26.6 3.6 %copy-start.1 = (bf16[642,512]{1,0:T(8,128)(2,1)S(1)}, bf16[642,512]{1,0:T(8,128)(2,1)}, u32[]{:S(2)}) copy-start(bf16[642,512]{1,0:T(8,128)(2,1)} %param.26) | copy-start | bytes 1972228
  26.6 3.6 %copy-start.3 = (bf16[512,512]{1,0:T(8,128)(2,1)S(1)}, bf16[512,512]{1,0:T(8,128)(2,1)}, u32[]{:S(2)}) copy-start(bf16[512,512]{1,0:T(8,128)(2,1)} %param.37) | copy-start | bytes 1572868
  34.2 1.9 %copy-start.10 = (bf16[512,512]{1,0:T(8,128)(2,1)S(1)}, bf16[512,512]{1,0:T(8,128)(2,1)}, u32[]{:S(2)}) copy-start(bf16[512,512]{1,0:T(8,128)(2,1)} %param.40) | copy-start | bytes 1572868
  34.2 3.5 %copy-start.6 = (s32[512]{0:T(512)S(1)}, s32[512]{0:T(512)}, u32[]{:S(2)}) copy-start(s32[512]{0:T(512)} %param.27) | copy-start | bytes 6148
  34.2 3.5 %copy-start.8 = (s32[2,1,128]{2,1,0:T(1,128)S(1)}, s32[2,1,128]{2,1,0:T(1,128)}, u32[]{:S(2)}) copy-start(s32[2,1,128]{2,1,0:T(1,128)} %get-tuple-element.8) | copy-start | bytes 3076
  34.2 3.5 %copy-start.4 = (bf16[512,512]{1,0:T(8,128)(2,1)S(1)}, bf16[512,512]{1,0:T(8,128)(2,1)}, u32[]{:S(2)}) copy-start(bf16[512,512]{1,0:T(8,128)(2,1)} %refs_0_.1) | copy-start | bytes 1572868
  34.2 3.5 %copy-start.12 = (bf16[256,512]{1,0:T(8,128)(2,1)S(1)}, bf16[256,512]{1,0:T(8,128)(2,1)}, u32[]{:S(2)}) copy-start(bf16[256,512]{1,0:T(8,128)(2,1)} %get-tuple-element.7) | copy-start | bytes 786436
  36.0 1.8 %copy-start.2 = (bf16[642,512]{1,0:T(8,128)(2,1)}, bf16[642,512]{1,0:T(8,128)(2,1)S(1)}, u32[]{:S(2)}) copy-start(bf16[642,512]{1,0:T(8,128)(2,1)S(1)} %add_convert_fusion.1) | copy-start | bytes 1972228
  37.7 6.6 %copy-start.7 = (bf16[160,512]{1,0:T(8,128)(2,1)}, bf16[160,512]{1,0:T(8,128)(2,1)S(1)}, u32[]{:S(2)}) copy-start(bf16[160,512]{1,0:T(8,128)(2,1)S(1)} %fusion.13) | copy-start | bytes 491524
  37.7 1.8 %copy-start.13 = (s32[3072]{0:T(1024)S(1)}, s32[3072]{0:T(1024)}, u32[]{:S(2)}) copy-start(s32[3072]{0:T(1024)} %param.31) | copy-start | bytes 36868
  39.5 4.8 %copy-start.11 = (bf16[512,512]{1,0:T(8,128)(2,1)S(1)}, bf16[512,512]{1,0:T(8,128)(2,1)}, u32[]{:S(2)}) copy-start(bf16[512,512]{1,0:T(8,128)(2,1)} %param.42) | copy-start | bytes 1572868
  44.3 0.7 %copy-start.14 = (s32[3072]{0:T(1024)S(1)}, s32[3072]{0:T(1024)}, u32[]{:S(2)}) copy-start(s32[3072]{0:T(1024)} %param.30) | copy-start | bytes 36868
  53.0 1.6 %copy-start.5 = (bf16[512,512]{1,0:T(8,128)(2,1)S(1)}, bf16[512,512]{1,0:T(8,128)(2,1)}, u32[]{:S(2)}) copy-start(bf16[512,512]{1,0:T(8,128)(2,1)} %param.45) | copy-start | bytes 1572868

commit v2 on v1

--- a/solution.py
+++ b/solution.py
@@ -16,35 +16,6 @@
 
 def normed(values):
     return values / jnp.sqrt(jnp.mean(values * values, axis=-1, keepdims=True) + EPSILON)
-
-
-def node_update(latent, incoming, first, second, third):
-    hidden = jax.nn.silu(product(latent, first) + product(incoming, second)).astype(jnp.bfloat16)
-    return (latent.astype(jnp.float32) + normed(product(hidden, third))).astype(jnp.bfloat16)
-
-
-def selector_rows(row_ids, width):
-    columns = lax.broadcasted_iota(jnp.int32, (row_ids.shape[0], width), 1)
-    return (columns == row_ids[:, None]).astype(jnp.bfloat16)
-
-
-def edge_update(
-    node_table, lifted, source, target, edge_w_src, edge_w_dst, edge_w2, node_w1, node_w2, node_w3
-):
-    fine_count = lifted.shape[0]
-    sender = product(node_table, edge_w_src).astype(jnp.bfloat16)
-    receiver = product(lifted, edge_w_dst).astype(jnp.bfloat16)
-    source_pick = selector_rows(source, node_table.shape[0])
-    target_pick = selector_rows(target, fine_count)
-    edge_sum = product(source_pick, sender) + product(target_pick, receiver)
-    edge_hidden = jax.nn.silu(edge_sum).astype(jnp.bfloat16)
-    hidden_sums = lax.dot_general(
-        target_pick, edge_hidden, (((0,), (0,)), ((), ())), preferred_element_type=jnp.float32
-    )
-    leading = hidden_sums.astype(jnp.bfloat16)
-    rest = (hidden_sums - leading.astype(jnp.float32)).astype(jnp.bfloat16)
-    aggregate = product(leading, edge_w2) + product(rest, edge_w2)
-    return node_update(lifted, aggregate.astype(jnp.bfloat16), node_w1, node_w2, node_w3)
 
 
 def one_hot(ids, axis, shape):
@@ -351,6 +322,188 @@
     )
 
 
+def gate(values):
+    return values * (0.5 + 0.5 * jnp.tanh(0.5 * values))
+
+
+def tail_kernel(
+    groups,
+    tiles,
+    ups_ref,
+    ids_ref,
+    rim_ref,
+    rim_parent_ref,
+    fine_parent_ref,
+    source_ref,
+    target_ref,
+    coarse_ref,
+    fine_ref,
+    w_coarse_ref,
+    c1_ref,
+    c2_ref,
+    c3_ref,
+    descend_ref,
+    w_fine_ref,
+    src_w_ref,
+    dst_w_ref,
+    e2_ref,
+    n1_ref,
+    n2_ref,
+    n3_ref,
+    fine_out_ref,
+    mid_out_ref,
+    coarse_out_ref,
+    fine_v,
+    weights_v,
+    coarse_v,
+    near_v,
+    down_v,
+    table_v,
+    sent_v,
+    got_v,
+    sums_v,
+    load_sem,
+):
+    bf16, f32 = (jnp.bfloat16, jnp.float32)
+    me = lax.axis_index("rhombus") * tiles + lax.axis_index("tile")
+    devices, mids, features = ups_ref.shape
+    fines = fine_v.shape[0]
+    coarse_count = coarse_ref.shape[0]
+    rims = rim_ref.shape[0] // 2
+    reach = min(5, devices)
+    names = [
+        w_coarse_ref, c1_ref, c2_ref, c3_ref, descend_ref, w_fine_ref,
+        src_w_ref, dst_w_ref, e2_ref, n1_ref, n2_ref, n3_ref,
+    ]
+    loads = [pltpu.make_async_copy(ref, weights_v.at[i], load_sem.at[i]) for i, ref in enumerate(names)]
+    loads.insert(6, pltpu.make_async_copy(fine_ref, fine_v, load_sem.at[len(names)]))
+    for load in loads:
+        load.start()
+
+    def weight(i):
+        loads[i if i < 6 else i + 1].wait()
+        return weights_v[i]
+
+    mid_all = ups_ref[...].reshape(devices * mids, features)
+    mid_msg = product(mid_all, weight(0)).astype(bf16)
+    id_row = jnp.concatenate([ids_ref[d][:, :mids] for d in range(devices)], axis=1)
+    coarse_in = product(one_hot(id_row, 0, (coarse_count, devices * mids)), mid_msg).astype(bf16)
+    coarse = coarse_ref[...]
+    hidden = gate(product(coarse, weight(1)) + product(coarse_in, weight(2))).astype(bf16)
+    updated = (coarse.astype(f32) + normed(product(hidden, weight(3)))).astype(bf16)
+    coarse_out_ref[...] = updated
+    padded = coarse_v.shape[0]
+    edge = coarse_count // 16 * 16
+    coarse_v[edge:] = jnp.zeros((padded - edge, features), bf16)
+    coarse_v[:coarse_count] = updated
+
+    low = jnp.clip(me - 2, 0, devices - reach)
+    near = near_v.shape[0]
+    window = reach * mids
+    spare = down_v.shape[0] - window
+    near_row = jnp.concatenate(
+        [ids_ref[low + d][:, :mids] for d in range(reach)] + [jnp.zeros((1, spare), jnp.int32)], axis=1
+    )
+    pick = one_hot(as_columns(near_row, padded)[:window], 1, (window, padded))
+    picked = product(pick, coarse_v[...]).astype(bf16)
+    down = product(picked, weight(4)).astype(bf16)
+    near_up = ups_ref[pl.ds(low, reach)].reshape(window, features)
+    near_out = (near_up.astype(f32) + down.astype(f32)).astype(bf16)
+    near_v[...] = near_out.reshape(reach, mids, features)
+    mid_out_ref[...] = near_v[me - low]
+    down_v[:window] = product(near_out, weight(5)).astype(bf16)
+    down_v[window:] = jnp.zeros((spare, features), bf16)
+
+    parents = fine_parent_ref[...]
+    side = parents // mids
+    shift = jnp.where(side == 1, -1, jnp.where(side == 2, 1, 0))
+    own_parent = (me + shift) * mids + parents % mids
+    table_parent = jnp.concatenate([own_parent, rim_parent_ref[0], rim_parent_ref[1]], axis=1)
+    table_parent = jnp.where(table_parent < 0, -1, table_parent - low * mids)
+    width = down_v.shape[0]
+    lift = one_hot(as_columns(table_parent, width), 1, (fines + 2 * rims, width))
+    raised = product(lift, down_v[...])
+    loads[6].wait()
+    table_v[:fines] = (fine_v[...].astype(f32) + raised[:fines]).astype(bf16)
+    table_v[fines:] = (rim_ref[...].astype(f32) + raised[fines:]).astype(bf16)
+
+    across = (((1,), (1,)), ((), ()))
+
+    def flipped(w, rows):
+        return lax.dot_general(jnp.transpose(w), rows, across, preferred_element_type=f32).astype(bf16)
+
+    lifted = table_v[:fines]
+    sent_v[...] = flipped(weight(6), table_v[...])
+    got_v[...] = flipped(weight(7), lifted)
+    sums_v[...] = jnp.zeros(sums_v.shape, f32)
+    edges = source_ref.shape[1]
+    step = next(size for size in (1024, 512, 256, 128) if edges % size == 0)
+
+    def block(i, carry):
+        at = pl.ds(pl.multiple_of(i * step, step), step)
+        source_pick = one_hot(source_ref[:, at], 0, (fines + 2 * rims, step))
+        target_pick = one_hot(target_ref[:, at], 0, (fines, step))
+        edge_sum = product(sent_v[...], source_pick) + product(got_v[...], target_pick)
+        edge_hidden = gate(edge_sum).astype(bf16)
+        sums_v[...] += lax.dot_general(target_pick, edge_hidden, across, preferred_element_type=f32)
+        return carry
+
+    lax.fori_loop(0, edges // step, block, 0)
+    sums = sums_v[...]
+    leading = sums.astype(bf16)
+    rest = (sums - leading.astype(f32)).astype(bf16)
+    e2 = weight(8)
+    aggregate = (product(leading, e2) + product(rest, e2)).astype(bf16)
+    hidden = gate(product(lifted, weight(9)) + product(aggregate, weight(10))).astype(bf16)
+    fine_out_ref[...] = (lifted.astype(f32) + normed(product(hidden, weight(11)))).astype(bf16)
+
+
+def finished(ups, ids, rim, rim_parent, fine_latent, coarse_latent, fine_parent, edge_source, edge_target, weights):
+    groups, tiles = (lax.axis_size("rhombus"), lax.axis_size("tile"))
+    devices, mids, features = ups.shape
+    fines = fine_latent.shape[0]
+    halos = rim.shape[0]
+    bf16, f32 = (jnp.bfloat16, jnp.float32)
+    vmem = pl.BlockSpec(memory_space=pltpu.VMEM)
+    hbm = pl.BlockSpec(memory_space=pl.ANY)
+    reach = min(5, devices)
+    ceil = lambda n: -(-n // 128) * 128
+    return pl.pallas_call(
+        lambda *refs: tail_kernel(groups, tiles, *refs),
+        out_shape=(
+            jax.ShapeDtypeStruct(fine_latent.shape, bf16),
+            jax.ShapeDtypeStruct((mids, features), bf16),
+            jax.ShapeDtypeStruct(coarse_latent.shape, bf16),
+        ),
+        in_specs=[vmem] * 8 + [hbm] * (1 + len(weights)),
+        out_specs=(vmem, vmem, vmem),
+        scratch_shapes=[
+            pltpu.VMEM(fine_latent.shape, bf16),
+            pltpu.VMEM((len(weights), features, features), bf16),
+            pltpu.VMEM((ceil(coarse_latent.shape[0]), features), bf16),
+            pltpu.VMEM((reach, mids, features), bf16),
+            pltpu.VMEM((ceil(reach * mids), features), bf16),
+            pltpu.VMEM((fines + halos, features), bf16),
+            pltpu.VMEM((features, fines + halos), bf16),
+            pltpu.VMEM((features, fines), bf16),
+            pltpu.VMEM((fines, features), f32),
+            pltpu.SemaphoreType.DMA((len(weights) + 1,)),
+        ],
+        name="tail",
+    )(
+        ups,
+        ids,
+        rim,
+        rim_parent,
+        fine_parent[None, :],
+        edge_source[None, :],
+        edge_target[None, :],
+        coarse_latent,
+        fine_latent,
+        *weights,
+    )
+
+
 def on_device(
     fine_latent,
     mid_latent,
@@ -377,45 +530,16 @@
     node_w2,
     node_w3,
 ):
-    mid_count = mid_latent.shape[0]
-    coarse_count = coarse_latent.shape[0]
-    rim_count = halo_rows.shape[0] // 2
-    tiles = lax.axis_size("tile")
-    me = lax.axis_index("rhombus") * tiles + lax.axis_index("tile")
     ups, ids, rim, rim_parent = gathered(
         fine_latent, mid_latent, fine_parent, mid_parent, halo_rows, w_child, mid_w1, mid_w2, mid_w3
     )
-    mid_all = ups.reshape(-1, ups.shape[-1])
-    id_all = ids[:, 0, :mid_count].reshape(-1)
-    mid_msg = product(mid_all, w_coarse).astype(jnp.bfloat16)
-    coarse_ids = lax.broadcasted_iota(jnp.int32, (coarse_count, id_all.shape[0]), 0)
-    selector = (coarse_ids == id_all[None, :]).astype(jnp.bfloat16)
-    coarse_in = product(selector, mid_msg).astype(jnp.bfloat16)
-    coarse_out = node_update(coarse_latent, coarse_in, coarse_w1, coarse_w2, coarse_w3)
-    reach = min(5 * mid_count, id_all.shape[0])
-    low = jnp.clip((me - 2) * mid_count, 0, id_all.shape[0] - reach)
-    near_up = lax.dynamic_slice_in_dim(mid_all, low, reach, 0)
-    near_id = lax.dynamic_slice_in_dim(id_all, low, reach, 0)
-    picked = product(selector_rows(near_id, coarse_count), coarse_out).astype(jnp.bfloat16)
-    down = product(picked, w_descend).astype(jnp.bfloat16)
-    near_out = (near_up.astype(jnp.float32) + down.astype(jnp.float32)).astype(jnp.bfloat16)
-    mid_out = lax.dynamic_slice_in_dim(near_out, me * mid_count - low, mid_count, 0)
-    fine_down = product(near_out, w_fine).astype(jnp.bfloat16)
-    side = fine_parent // mid_count
-    shift = jnp.where(side == 1, -1, jnp.where(side == 2, 1, 0))
-    own_parent = (me + shift) * mid_count + fine_parent % mid_count
-    table_parent = jnp.concatenate([own_parent, rim_parent.reshape(-1)]) - low
-    table_parent = jnp.where(
-        jnp.concatenate([own_parent, rim_parent.reshape(-1)]) < 0, -1, table_parent
-    )
-    raised = product(selector_rows(table_parent, reach), fine_down)
-    node_table = (jnp.concatenate([fine_latent, rim], axis=0).astype(jnp.float32) + raised).astype(jnp.bfloat16)
-    lifted = node_table[: fine_latent.shape[0]]
-    fine_out = edge_update(
-        node_table,
-        lifted,
-        edge_source,
-        edge_target,
+    weights = (
+        w_coarse,
+        coarse_w1,
+        coarse_w2,
+        coarse_w3,
+        w_descend,
+        w_fine,
         edge_w_src,
         edge_w_dst,
         edge_w2,
@@ -423,7 +547,9 @@
         node_w2,
         node_w3,
     )
-    return (fine_out, mid_out, coarse_out)
+    return finished(
+        ups, ids, rim, rim_parent, fine_latent, coarse_latent, fine_parent, edge_source, edge_target, weights
+    )
 
 
 def solution(mesh):

time: 64.3 us -> 44.4 us (0.69)
  matrix products: 32.1 us -> 0 us
  Pallas kernels: 23.8 us -> 42.3 us
  local copies, waits for them, and re-layouts: 4.11 us -> 1.16 us
  other arithmetic: 2.75 us -> 0 us
    dot_general x12 -> x0, matrix products: 32.1 us -> none  [the longest x11 24.1 us: product(): return jnp.dot(left, right, preferred_element_type=jnp.float32)]
    pallas_call x0 -> x1, Pallas kernels: none -> 18.5 us  [finished(): pl.pallas_call(lambda *refs: tail_kernel(groups, tiles, *refs), out_shape...]
    convert_element_type x2 -> x0, other arithmetic: 2.71 us -> none  [node_update(): (latent.astype(jnp.float32) + normed(product(hidden, third))).astype(jnp....]
    dynamic_slice x2 -> x0, local copies, waits for them, and re-layouts: 1.48 us -> none  [the longest x1 1.4 us: on_device(): lax.dynamic_slice_in_dim(near_out, me * mid_count - low, mid_count, 0)]
    slice x1 -> x0, local copies, waits for them, and re-layouts: 0.76 us -> none  [on_device(): id_all = ids[:, 0, :mid_count].reshape(-1)]
    pad x1, local copies, waits for them, and re-layouts: 1.26 us -> 0.51 us  [gathered(): coarse_ids = jnp.pad(mid_parent[None, :], ((0, 0), (0, width - mids)))]
where the time goes in v2:
time: 44.4 us; the launch traced here: 44.1 us
  Pallas kernels  42.3 us (95%)
  local copies, waits for them, and re-layouts  1.16 us (3%)
  between operations  0.65 us (1%)
    pallas_call x1, Pallas kernels, gathered(): pl.pallas_call(lambda *refs: gather_kernel(groups, tiles, *refs), out_sha...  23.8 us
    pallas_call x1, Pallas kernels, finished(): pl.pallas_call(lambda *refs: tail_kernel(groups, tiles, *refs), out_shape...  18.5 us

profile of v2, /device:TPU:11, one launch (start us, length us, event | category | flops | bytes accessed | tf_op | source)
XLA Modules:
  0.0 44.1 jit_solution(5364824510346015189)
XLA Ops:
  0.6 0.0 copy-start
  0.6 0.6 %copy-done = s32[32]{0:T(128)S(1)} copy-done((s32[32]{0:T(128)S(1)}, s32[32]{0:T(128)}, u32[]{:S(2)}) %copy-start) | copy-done | bytes 152
  1.3 0.5 %pad.4.refs_4_ = s32[1,128]{1,0:T(1,128)} pad(s32[1,32]{1,0:T(1,128)S(1)} %bitcast.10, s32[]{:T(128)} %constant.0.clone.1), padding=0_0x0_96 | pad | bytes 644 | tf_op jit(solution)/shard_map/jit(_pad)/pad | solution.py:274
  1.8 23.8 %gather_mids.1 = (bf16[32,32,512]{2,1,0:T(8,128)(2,1)}, s32[32,1,128]{2,1,0:T(1,128)}, bf16[256,512]{1,0:T(8,128)(2,1)}, s32[2,1,128]{2,1,0:T(1,128)}) custom-call(bf16[512,512]{1,0:T(8,128)(2,1)} %refs_8_.3, s32[1,512]{1,0:T(1,128)} %bitcast.7, s32[1,256]{1,0:T(1,128)} %bitcast.9, bf16[32,512]{1,0:T(8,128)(2,1)} %refs_3_.1, s32[1,128]{1,0:T(1,128)} %pad.4.refs_4_, ...), custom_call_target="tpu_custom_call" | custom-call | tf_op jit(solution)/shard_map/gather_mids/pallas_call | solution.py:283
  25.6 18.5 %tail.1 = (bf16[512,512]{1,0:T(8,128)(2,1)}, bf16[32,512]{1,0:T(8,128)(2,1)}, bf16[642,512]{1,0:T(8,128)(2,1)}) custom-call(bf16[32,32,512]{2,1,0:T(8,128)(2,1)} %get-tuple-element.7.refs_0_, s32[32,1,128]{2,1,0:T(1,128)} %get-tuple-element.8.refs_1_, bf16[256,512]{1,0:T(8,128)(2,1)} %get-tuple-element.9.refs_2_, s32[2,1,128]{2,1,0:T(1,128)} %get-tuple-element.10.refs_3_, ...), custom_call_target="tpu_custom_call" | custom-call | tf_op jit(solution)/shard_map/tail/pallas_call | solution.py:471
Async XLA Ops:
  0.6 0.7 %copy-start = (s32[32]{0:T(128)S(1)}, s32[32]{0:T(128)}, u32[]{:S(2)}) copy-start(s32[32]{0:T(128)} %param.28) | copy-start | bytes 388

commit v3 on v1

v3 whole, which is shorter than its diff:
```python
import jax
import jax.numpy as jnp
from jax import lax
from jax.experimental import pallas as pl
from jax.experimental.pallas import tpu as pltpu
from jax.sharding import PartitionSpec as P

MESH = pl.DeviceIdType.MESH

EPSILON = 1e-05


def product(left, right):
    return jnp.dot(left, right, preferred_element_type=jnp.float32)


def normed(values):
    return values / jnp.sqrt(jnp.mean(values * values, axis=-1, keepdims=True) + EPSILON)


def gate(values):
    return values * (0.5 + 0.5 * jnp.tanh(0.5 * values))


def one_hot(ids, axis, shape):
    return jnp.where(lax.broadcasted_iota(jnp.int32, shape, axis) == ids, 1.0, 0.0).astype(jnp.bfloat16)


def as_columns(row, width):
    count = row.shape[1]
    column = jnp.transpose(jnp.broadcast_to(row, (128, count)))
    return jnp.concatenate([column] * (width // 128), axis=1)


def sweep_kernel(
    groups,
    tiles,
    parent_ref,
    halo_ref,
    latent_ref,
    coarse_id_ref,
    source_ref,
    target_ref,
    coarse_ref,
    fine_ref,
    *rest_refs,
):
    weight_refs = rest_refs[:16]
    fine_out_ref, mid_out_ref, coarse_out_ref = rest_refs[16:19]
    ups_ref, ids_ref, rim_ref, rim_parent_ref, fine_v, weights_v = rest_refs[19:25]
    sums_v, beside_v, picked_v, picked_parent_v, kept_v, flip_v, into_v = rest_refs[25:32]
    coarse_v, down_v, table_v, sent_v, got_v, edge_v = rest_refs[32:38]
    load_sem, near_send, near_recv, tree_send, block_recv, id_recv = rest_refs[38:]
    group, tile = (lax.axis_index("rhombus"), lax.axis_index("tile"))
    pairs = tiles // 2
    pair, core = (tile // 2, tile % 2)
    mids = latent_ref.shape[0]
    rims = halo_ref.shape[1] // 2
    fines, features = fine_ref.shape

    bf16, f32 = (jnp.bfloat16, jnp.float32)
    loads = [pltpu.make_async_copy(fine_ref, fine_v, load_sem.at[len(weight_refs)])]
    loads += [pltpu.make_async_copy(ref, weights_v.at[i], load_sem.at[i]) for i, ref in enumerate(weight_refs)]
    for load in loads:
        load.start()

    def weight(i):
        loads[i + 1].wait()
        return weights_v[i]

    def at(group_id, pair_id, core_id):
        return (group_id, pair_id * 2 + core_id)

    columns = [at((group + k) % groups, pair, core) for k in range(1, groups)]
    if pairs == 4:
        across, along = (pair + 1 - 2 * (pair % 2), (pair + 2) % 4)
        corner = (across + 2) % 4
        level = [across, along]
    else:
        level = [(pair + k) % pairs for k in range(1, pairs)]
    row_peers = [at(group, other, core) for other in level]
    partner = at(group, pair, 1 - core)
    peers = columns + row_peers + [partner]

    barrier = pltpu.get_barrier_semaphore()
    for peer in peers:
        pl.semaphore_signal(barrier, inc=1, device_id=peer, device_id_type=MESH)

    @pl.when(tile > 0)
    def _():
        pl.semaphore_signal(barrier, inc=1, device_id=(group, tile - 1), device_id_type=MESH)

    @pl.when(tile < tiles - 1)
    def _():
        pl.semaphore_signal(barrier, inc=1, device_id=(group, tile + 1), device_id_type=MESH)

    me = group * tiles + tile
    halves = groups * pairs

    def place_of(group_id, pair_id, core_id):
        return core_id * halves + group_id * pairs + pair_id

    mine = place_of(group, pair, core)
    ids_ref[mine] = coarse_id_ref[...]
    loads[0].wait()
    fine = fine_v[...]
    parents = parent_ref[...]
    picker = one_hot(parents, 0, (3 * mids, fines))
    sums_v[...] = product(picker, fine)
    pl.semaphore_wait(barrier, len(peers) + 1 + (tile + tiles - 1) // tiles - (tile + 1) // tiles)

    def near(index, source, target, device):
        return pltpu.make_async_remote_copy(
            src_ref=source,
            dst_ref=target,
            send_sem=near_send.at[index],
            recv_sem=near_recv.at[index],
            device_id=device,
            device_id_type=MESH,
        )

    before, after = ((group, tile - 1), (group, tile + 1))
    to_before = [
        near(0, sums_v.at[pl.ds(mids, mids)], beside_v.at[0], before),
        near(1, picked_v.at[pl.ds(0, rims)], rim_ref.at[pl.ds(rims, rims)], before),
        near(2, picked_parent_v.at[0], rim_parent_ref.at[1], before),
    ]
    to_after = [
        near(3, sums_v.at[pl.ds(2 * mids, mids)], beside_v.at[1], after),
        near(4, picked_v.at[pl.ds(rims, rims)], rim_ref.at[pl.ds(0, rims)], after),
        near(5, picked_parent_v.at[1], rim_parent_ref.at[0], after),
    ]

    @pl.when(tile > 0)
    def _():
        to_before[0].start()

    @pl.when(tile < tiles - 1)
    def _():
        to_after[0].start()

    halo = halo_ref[...]
    picked_v[...] = product(one_hot(as_columns(halo, fines), 1, (2 * rims, fines)), fine).astype(jnp.bfloat16)
    side = parents // mids
    shift = jnp.where(side == 1, -1, jnp.where(side == 2, 1, 0))
    global_parents = (me + shift) * mids + parents % mids
    parent_column = jnp.transpose(jnp.broadcast_to(global_parents, (128, fines)))
    for half in range(2):
        hit = lax.broadcasted_iota(jnp.int32, (fines, rims), 0) == halo[:, half * rims : (half + 1) * rims]
        spread = jnp.concatenate([parent_column] * (rims // 128), axis=1)
        picked_parent_v[half] = jnp.sum(jnp.where(hit, spread, 0), axis=0, keepdims=True)

    @pl.when(tile > 0)
    def _():
        to_before[1].start()
        to_before[2].start()

    @pl.when(tile < tiles - 1)
    def _():
        to_after[1].start()
        to_after[2].start()

    child_w = weight(0)
    kept = product(latent_ref[...], weight(1))

    @pl.when(tile > 0)
    def _():
        to_after[0].wait_recv()

    @pl.when(tile == 0)
    def _():
        beside_v[1] = jnp.zeros_like(beside_v[1])
        rim_ref[pl.ds(0, rims)] = jnp.zeros((rims, rim_ref.shape[1]), rim_ref.dtype)
        rim_parent_ref[0] = jnp.full(rim_parent_ref.shape[1:], -1, jnp.int32)

    @pl.when(tile < tiles - 1)
    def _():
        to_before[0].wait_recv()

    @pl.when(tile == tiles - 1)
    def _():
        beside_v[0] = jnp.zeros_like(beside_v[0])
        rim_ref[pl.ds(rims, rims)] = jnp.zeros((rims, rim_ref.shape[1]), rim_ref.dtype)
        rim_parent_ref[1] = jnp.full(rim_parent_ref.shape[1:], -1, jnp.int32)

    total = sums_v[pl.ds(0, mids)] + beside_v[0] + beside_v[1]
    leading = total.astype(jnp.bfloat16)
    rest = (total - leading.astype(jnp.float32)).astype(jnp.bfloat16)
    mid_in = (product(leading, child_w) + product(rest, child_w)).astype(jnp.bfloat16)
    hidden = gate(kept + product(mid_in, weight(2))).astype(jnp.bfloat16)
    mid_up = latent_ref[...].astype(jnp.float32) + normed(product(hidden, weight(3)))
    ups_ref[mine] = mid_up.astype(jnp.bfloat16)

    started = []

    def copies(slot, index, device):
        return [
            pltpu.make_async_remote_copy(
                src_ref=held.at[slot],
                dst_ref=held.at[slot],
                send_sem=tree_send.at[kind, index],
                recv_sem=sems.at[slot],
                device_id=device,
                device_id_type=MESH,
            )
            for kind, (held, sems) in enumerate([(ups_ref, block_recv), (ids_ref, id_recv)])
        ]

    def send(slot, devices):
        for device in devices:
            for copy in copies(slot, len(started) // 2, device):
                copy.start()
                started.append(copy)

    def arrive(slot):
        for copy in copies(slot, 0, partner):
            copy.wait_recv()

    def slot_of(k, pair_id, core_id):
        return place_of((group + k) % groups, pair_id, core_id)

    order = [0] + sorted(range(1, groups), key=lambda k: min(k, groups - k))
    send(mine, columns + row_peers + [partner])
    coarse = coarse_ref[...]
    kept_v[...] = product(coarse, weight(4))
    flip_v[0] = jnp.transpose(weight(5))
    flip_v[1] = jnp.transpose(weight(6))
    for k in order:
        if k > 0:
            slot = slot_of(k, pair, core)
            arrive(slot)
            send(slot, row_peers + [partner])
    for n, k in enumerate(order):
        for place, other in enumerate(level):
            slot = slot_of(k, other, core)
            arrive(slot)
            onward = [partner]
            if pairs == 4 and n % 2 == place:
                onward = [at(group, level[1 - place], core), partner]
            send(slot, onward)
    if pairs == 4:
        for k in order:
            slot = slot_of(k, corner, core)
            arrive(slot)
            send(slot, [partner])
    w_coarse = weight(7)
    coarse_count = coarse.shape[0]

    def half_sum(half):
        held = pl.ds(half * halves, halves)
        mid_msg = product(ups_ref[held].reshape(halves * mids, features), w_coarse).astype(bf16)
        id_row = jnp.concatenate([ids_ref[half * halves + d][:, :mids] for d in range(halves)], axis=1)
        return product(one_hot(id_row, 0, (coarse_count, halves * mids)), mid_msg)

    into_v[...] = half_sum(core)
    for k in order:
        for other in range(pairs):
            arrive(slot_of(k, other, 1 - core))

    @pl.when(tile > 0)
    def _():
        for copy in to_after[1:]:
            copy.wait_recv()

    @pl.when(tile < tiles - 1)
    def _():
        for copy in to_before[1:]:
            copy.wait_recv()

    coarse_in = (into_v[...] + half_sum(1 - core)).astype(bf16)
    hidden = gate(kept_v[...] + product(coarse_in, weight(8))).astype(bf16)
    updated = (coarse.astype(f32) + normed(product(hidden, weight(9)))).astype(bf16)
    coarse_out_ref[...] = updated
    padded = coarse_v.shape[0]
    edge = coarse_count // 16 * 16
    coarse_v[edge:] = jnp.zeros((padded - edge, features), bf16)
    coarse_v[:coarse_count] = updated

    nearby = []
    for d in range(-2, 3):
        other = (me + d + 2 * groups * tiles) % (groups * tiles)
        other_tile = other % tiles
        nearby.append(place_of(other // tiles, other_tile // 2, other_tile % 2))
    window = len(nearby) * mids
    spare = down_v.shape[0] - window
    near_row = jnp.concatenate(
        [ids_ref[slot][:, :mids] for slot in nearby] + [jnp.zeros((1, spare), jnp.int32)], axis=1
    )
    pick = one_hot(as_columns(near_row, padded)[:window], 1, (window, padded))
    picked = product(pick, coarse_v[...]).astype(bf16)
    down = product(picked, weight(10)).astype(bf16)
    near_up = jnp.concatenate([ups_ref[slot] for slot in nearby], axis=0)
    near_out = (near_up.astype(f32) + down.astype(f32)).astype(bf16)
    mid_out_ref[...] = near_out[2 * mids : 3 * mids]
    down_v[:window] = product(near_out, weight(11)).astype(bf16)
    down_v[window:] = jnp.zeros((spare, features), bf16)

    own_parent = (2 + shift) * mids + parents % mids
    far_parent = jnp.concatenate([rim_parent_ref[0], rim_parent_ref[1]], axis=1)
    far_parent = jnp.where(far_parent < 0, -1, far_parent - (me - 2) * mids)
    table_parent = jnp.concatenate([own_parent, far_parent], axis=1)
    width = down_v.shape[0]
    lift = one_hot(as_columns(table_parent, width), 1, (fines + 2 * rims, width))
    raised = product(lift, down_v[...])
    table_v[:fines] = (fine.astype(f32) + raised[:fines]).astype(bf16)
    table_v[fines:] = (rim_ref[...].astype(f32) + raised[fines:]).astype(bf16)

    across = (((1,), (1,)), ((), ()))

    def flipped(w, rows):
        return lax.dot_general(w, rows, across, preferred_element_type=f32).astype(bf16)

    lifted = table_v[:fines]
    sent_v[...] = flipped(flip_v[0], table_v[...])
    got_v[...] = flipped(flip_v[1], lifted)
    edge_v[...] = jnp.zeros(edge_v.shape, f32)
    edges = source_ref.shape[1]
    step = next(size for size in (1024, 512, 256, 128) if edges % size == 0)

    def block(i, carry):
        at = pl.ds(pl.multiple_of(i * step, step), step)
        source_pick = one_hot(source_ref[:, at], 0, (fines + 2 * rims, step))
        target_pick = one_hot(target_ref[:, at], 0, (fines, step))
        edge_sum = product(sent_v[...], source_pick) + product(got_v[...], target_pick)
        edge_hidden = gate(edge_sum).astype(bf16)
        edge_v[...] += lax.dot_general(target_pick, edge_hidden, across, preferred_element_type=f32)
        return carry

    lax.fori_loop(0, edges // step, block, 0)
    sums = edge_v[...]
    leading = sums.astype(bf16)
    rest = (sums - leading.astype(f32)).astype(bf16)
    e2 = weight(12)
    aggregate = (product(leading, e2) + product(rest, e2)).astype(bf16)
    hidden = gate(product(lifted, weight(13)) + product(aggregate, weight(14))).astype(bf16)
    fine_out_ref[...] = (lifted.astype(f32) + normed(product(hidden, weight(15)))).astype(bf16)

    @pl.when(tile > 0)
    def _():
        for copy in to_before:
            copy.wait_send()

    @pl.when(tile < tiles - 1)
    def _():
        for copy in to_after:
            copy.wait_send()

    for copy in started:
        copy.wait_send()


def on_device(
    fine_latent,
    mid_latent,
    coarse_latent,
    fine_parent,
    mid_parent,
    halo_rows,
    edge_source,
    edge_target,
    w_child,
    mid_w1,
    mid_w2,
    mid_w3,
    w_coarse,
    coarse_w1,
    coarse_w2,
    coarse_w3,
    w_descend,
    w_fine,
    edge_w_src,
    edge_w_dst,
    edge_w2,
    node_w1,
    node_w2,
    node_w3,
):
    groups, tiles = (lax.axis_size("rhombus"), lax.axis_size("tile"))
    devices = groups * tiles
    fines, features = fine_latent.shape
    mids = mid_latent.shape[0]
    halos = halo_rows.shape[0]
    rims = halos // 2
    coarse_count = coarse_latent.shape[0]
    weights = (
        w_child,
        mid_w1,
        mid_w2,
        mid_w3,
        coarse_w1,
        edge_w_src,
        edge_w_dst,
        w_coarse,
        coarse_w2,
        coarse_w3,
        w_descend,
        w_fine,
        edge_w2,
        node_w1,
        node_w2,
        node_w3,
    )
    ceil = lambda n: -(-n // 128) * 128
    width = ceil(mids)
    coarse_ids = jnp.pad(mid_parent[None, :], ((0, 0), (0, width - mids)))
    pairs = tiles // 2
    level = 2 if pairs == 4 else pairs - 1
    sends = groups + level + (groups - 1) * (level + 1) + groups * level
    sends += 2 * groups if pairs == 4 else 0
    bf16, f32, i32 = (jnp.bfloat16, jnp.float32, jnp.int32)
    vmem = pl.BlockSpec(memory_space=pltpu.VMEM)
    hbm = pl.BlockSpec(memory_space=pl.ANY)
    dma = pltpu.SemaphoreType.DMA
    return pl.pallas_call(
        lambda *refs: sweep_kernel(groups, tiles, *refs),
        out_shape=(
            jax.ShapeDtypeStruct((fines, features), bf16),
            jax.ShapeDtypeStruct((mids, features), bf16),
            jax.ShapeDtypeStruct((coarse_count, features), bf16),
        ),
        in_specs=[vmem] * 7 + [hbm] * (1 + len(weights)),
        out_specs=(vmem, vmem, vmem),
        scratch_shapes=[
            pltpu.VMEM((devices, mids, features), bf16),
            pltpu.VMEM((devices, 1, width), i32),
            pltpu.VMEM((halos, features), bf16),
            pltpu.VMEM((2, 1, rims), i32),
            pltpu.VMEM((fines, features), bf16),
            pltpu.VMEM((len(weights), features, features), bf16),
            pltpu.VMEM((3 * mids, features), f32),
            pltpu.VMEM((2, mids, features), f32),
            pltpu.VMEM((halos, features), bf16),
            pltpu.VMEM((2, 1, rims), i32),
            pltpu.VMEM((coarse_count, features), f32),
            pltpu.VMEM((2, features, features), bf16),
            pltpu.VMEM((coarse_count, features), f32),
            pltpu.VMEM((ceil(coarse_count), features), bf16),
            pltpu.VMEM((ceil(5 * mids), features), bf16),
            pltpu.VMEM((fines + halos, features), bf16),
            pltpu.VMEM((features, fines + halos), bf16),
            pltpu.VMEM((features, fines), bf16),
            pltpu.VMEM((fines, features), f32),
            dma((len(weights) + 1,)),
            dma((6,)),
            dma((6,)),
            dma((2, sends)),
            dma((devices,)),
            dma((devices,)),
        ],
        compiler_params=pltpu.CompilerParams(collective_id=0, has_side_effects=True),
        name="sweep",
    )(
        fine_parent[None, :],
        halo_rows[None, :],
        mid_latent,
        coarse_ids,
        edge_source[None, :],
        edge_target[None, :],
        coarse_latent,
        fine_latent,
        *weights,
    )


def solution(mesh):
    placed = (
        P(("rhombus", "tile"), None),
        P(("rhombus", "tile"), None),
        P(),
        P(("rhombus", "tile")),
        P(("rhombus", "tile")),
        P(("rhombus", "tile")),
        P(("rhombus", "tile")),
        P(("rhombus", "tile")),
        P(),
        P(),
        P(),
        P(),
        P(),
        P(),
        P(),
        P(),
        P(),
        P(),
        P(),
        P(),
        P(),
        P(),
        P(),
        P(),
    )
    return jax.shard_map(
        on_device,
        mesh=mesh,
        in_specs=placed,
        out_specs=(P(("rhombus", "tile"), None), P(("rhombus", "tile"), None), P()),
        check_vma=False,
    )
```

time: 64.3 us -> 43.2 us (0.67)
  matrix products: 32.1 us -> 0 us
  Pallas kernels: 23.8 us -> 37.7 us
  other arithmetic: 2.75 us -> 0 us
    dot_general x12 -> x0, matrix products: 32.1 us -> none  [the longest x11 24.1 us: product(): return jnp.dot(left, right, preferred_element_type=jnp.float32)]
    pallas_call x1, Pallas kernels: 23.8 us -> 37.7 us  [on_device(): pl.pallas_call(lambda *refs: sweep_kernel(groups, tiles, *refs), out_shap...]
    unnamed x30 -> x9, local copies, waits for them, and re-layouts: 0.21 us -> 4.05 us
    convert_element_type x2 -> x0, other arithmetic: 2.71 us -> none  [node_update(): (latent.astype(jnp.float32) + normed(product(hidden, third))).astype(jnp....]
    dynamic_slice x2 -> x0, local copies, waits for them, and re-layouts: 1.48 us -> none  [the longest x1 1.4 us: on_device(): lax.dynamic_slice_in_dim(near_out, me * mid_count - low, mid_count, 0)]
    slice x1 -> x0, local copies, waits for them, and re-layouts: 0.76 us -> none  [on_device(): id_all = ids[:, 0, :mid_count].reshape(-1)]
    pad x1, local copies, waits for them, and re-layouts: 1.26 us -> 0.51 us  [on_device(): coarse_ids = jnp.pad(mid_parent[None, :], ((0, 0), (0, width - mids)))]
where the time goes in v3:
time: 43.2 us; the launch traced here: 43 us
  Pallas kernels  37.7 us (87%)
  local copies, waits for them, and re-layouts  4.56 us (11%)
  between operations  0.66 us (2%)
    pallas_call x1, Pallas kernels, on_device(): pl.pallas_call(lambda *refs: sweep_kernel(groups, tiles, *refs), out_shap...  37.7 us
    unnamed x9, local copies, waits for them, and re-layouts  4.05 us

profile of v3, /device:TPU:11, one launch (start us, length us, event | category | flops | bytes accessed | tf_op | source)
XLA Modules:
  0.0 43.0 jit_solution(1026441405738339458)
XLA Ops:
  0.6 0.0 copy-start.2
  0.6 0.6 %copy-done.2 = s32[32]{0:T(128)S(1)} copy-done((s32[32]{0:T(128)S(1)}, s32[32]{0:T(128)}, u32[]{:S(2)}) %copy-start.2) | copy-done | bytes 152
  1.3 0.5 %pad.4.refs_3_ = s32[1,128]{1,0:T(1,128)} pad(s32[1,32]{1,0:T(1,128)S(1)} %bitcast.9, s32[]{:T(128)} %constant.0.clone.1), padding=0_0x0_96 | pad | bytes 644 | tf_op jit(solution)/shard_map/jit(_pad)/pad | solution.py:405
  1.8 37.7 %sweep.1 = (bf16[512,512]{1,0:T(8,128)(2,1)}, bf16[32,512]{1,0:T(8,128)(2,1)}, bf16[642,512]{1,0:T(8,128)(2,1)}) custom-call(s32[1,512]{1,0:T(1,128)} %bitcast.7, s32[1,256]{1,0:T(1,128)} %bitcast.8, bf16[32,512]{1,0:T(8,128)(2,1)} %refs_2_.1, s32[1,128]{1,0:T(1,128)} %pad.4.refs_3_, s32[1,3072]{1,0:T(1,128)} %bitcast.5, s32[1,3072]{1,0:T(1,128)} %bitcast.6, ...), custom_call_target="tpu_custom_call" | custom-call | tf_op jit(solution)/shard_map/sweep/pallas_call | solution.py:414
  39.5 0.0 copy-start
  39.6 0.0 copy-start.1
  39.6 1.9 %copy.30 = bf16[512,512]{1,0:T(8,128)(2,1)} copy(bf16[512,512]{1,0:T(8,128)(2,1)} %get-tuple-element.6) | data formatting | bytes 1048576
  41.5 0.0 copy-done.1
  41.5 0.6 %copy.31 = bf16[32,512]{1,0:T(8,128)(2,1)} copy(bf16[32,512]{1,0:T(8,128)(2,1)S(1)} %copy-done.1) | data formatting | bytes 65536
  42.1 0.0 copy-done
  42.1 0.8 %copy.32 = bf16[642,512]{1,0:T(8,128)(2,1)} copy(bf16[642,512]{1,0:T(8,128)(2,1)S(1)} %copy-done) | data formatting | bytes 1314816
Async XLA Ops:
  0.6 0.7 %copy-start.2 = (s32[32]{0:T(128)S(1)}, s32[32]{0:T(128)}, u32[]{:S(2)}) copy-start(s32[32]{0:T(128)} %param.28) | copy-start | bytes 388
  39.5 2.6 %copy-start = (bf16[642,512]{1,0:T(8,128)(2,1)S(1)}, bf16[642,512]{1,0:T(8,128)(2,1)}, u32[]{:S(2)}) copy-start(bf16[642,512]{1,0:T(8,128)(2,1)} %get-tuple-element.8) | copy-start | bytes 1972228
  39.6 2.0 %copy-start.1 = (bf16[32,512]{1,0:T(8,128)(2,1)S(1)}, bf16[32,512]{1,0:T(8,128)(2,1)}, u32[]{:S(2)}) copy-start(bf16[32,512]{1,0:T(8,128)(2,1)} %get-tuple-element.7) | copy-start | bytes 98308
